TPU v7x, 1024 devices: a whole 4x4x32 slice. The times are simulated.
1024 devices in a mesh: seq: 128 (over y, z), head: 8 (over x, core).
Axes of the slice: x: 4, y: 4, z: 32, core: 2. Of those that a mesh axis runs over, the one named last changes fastest.
Arguments:
- queries: bfloat16 [16384, 3072], P('seq', 'head'), may hold values from -2 to 2
- key_rows: bfloat16 [16384, 3072], P('seq', 'head'), may hold values from -2 to 2
- values: bfloat16 [16384, 3072], P('seq', 'head'), may hold values from -6 to 6
- conv_input: bfloat16 [16384, 3072], P('seq', 'head'), may hold values from -0.14941406 to 0.14941406
- log_gates: bfloat16 [16384, 3072], P('seq', 'head'), may hold values from -1 to 0
- grad_output: bfloat16 [16384, 3072], P('seq', 'head'), may hold values from -0.8984375 to 0.8984375
- saved_state: float32 [128, 24, 128, 128], P('seq', 'head'), may hold values from -6 to 6
- conv_kernel: float32 [4, 3072], replicated, may hold values from -3 to 3
Outputs:
- grad_queries: bfloat16 [16384, 3072], P('seq', 'head')
- grad_keys: bfloat16 [16384, 3072], P('seq', 'head')
- grad_gates: bfloat16 [16384, 3072], P('seq', 'head')
- grad_input: bfloat16 [16384, 3072], P(('seq', 'head'))
- grad_kernel: float32 [4, 3072], P(None, 'head')
All inputs are finite; a program needn't handle non-finite values.
Results may differ from a plain program's by a relative error of at most 0.0049.
Values may be sent and summed in bfloat16 or wider, within the bound.
No kernel may reach another device: no remote copies, remote signals or barrier semaphores. Data moves between devices by JAX's collectives and lax.ppermute only.
A program may use at most 64 MiB of HBM per device.

v0:
```python
import jax
import jax.numpy as jnp
from jax import lax
from jax.sharding import PartitionSpec as P

DK = 128
DV = 128
STRETCH = 64


PRECISE = lax.Precision.HIGHEST


def prefix_2(x, axis, combine, identity):
    count, position = (lax.axis_size(axis), lax.axis_index(axis))
    everything = jax.tree.map(lambda part: lax.all_gather(part, axis), x)
    start = jax.tree.map(
        lambda part, zero: jnp.broadcast_to(jnp.asarray(zero, part.dtype), part.shape), x, identity
    )

    def hop(k, before):
        at = count - 1 - k
        reached = at > position
        new = combine(before, jax.tree.map(lambda part: part[at], everything))
        return jax.tree.map(lambda a, b: jnp.where(reached, a, b), new, before)

    return lax.fori_loop(0, count, hop, start)


def passed_along(x, axis, by):
    count = lax.axis_size(axis)
    pairs = [(i, i + by) for i in range(count) if 0 <= i + by < count]
    return lax.ppermute(x, axis, pairs)


def to_heads(array, head_count, width):
    length = array.shape[0]
    turned = array.reshape(length, head_count, width).transpose(1, 0, 2).astype(jnp.float32)
    return turned.reshape(head_count, length // STRETCH, STRETCH, width)


def from_heads(array):
    head_count, stretches, span, width = array.shape
    return (
        array.reshape(head_count, stretches * span, width)
        .transpose(1, 0, 2)
        .reshape(stretches * span, head_count * width)
    )


def linked_sequence(running_totals, summand_terms, beginning_position, backward_sweep):

    def step_forward(current, inputs):
        decays, addend = inputs
        return (jnp.exp(decays)[..., None] * current + addend, current)

    final, visited = lax.scan(
        step_forward,
        beginning_position,
        (jnp.moveaxis(running_totals, 1, 0), jnp.moveaxis(summand_terms, 1, 0)),
        reverse=backward_sweep,
    )
    return (final, jnp.moveaxis(visited, 0, 1))


def local_grads(
    grad_c, value_c, within, running_totals, query_up, key_down, key_tail, starts, ends
):
    steps_idx = jnp.arange(STRETCH)
    lower_mask = (steps_idx[:, None] >= steps_idx[None, :]).astype(jnp.float32)
    scores = jnp.einsum("hnte,hnse->hnts", grad_c, value_c, precision=PRECISE) * lower_mask
    grad_query = jnp.exp(within) * (
        jnp.einsum("hnte,hnae->hnta", grad_c, starts, precision=PRECISE)
        + jnp.einsum("hnts,hnsa->hnta", scores, key_down, precision=PRECISE)
    )
    grad_key = jnp.exp(-within) * jnp.einsum(
        "hnts,hnta->hnsa", scores, query_up, precision=PRECISE
    ) + jnp.exp(running_totals[:, :, None] - within) * jnp.einsum(
        "hnse,hnae->hnsa", value_c, ends, precision=PRECISE
    )
    weights = jnp.einsum("hnsa,hnta->hnst", key_down, query_up, precision=PRECISE) * lower_mask.T
    grad_value = jnp.einsum("hnst,hnte->hnse", weights, grad_c, precision=PRECISE) + jnp.einsum(
        "hnsa,hnae->hnse", key_tail, ends, precision=PRECISE
    )
    return (grad_query, grad_key, grad_value)


def compose(earlier, later):
    return (earlier[0] * later[0], later[0][..., None] * earlier[1] + later[1])


def per_device(
    queries, key_rows, values, conv_input, log_gates, grad_output, saved_state, conv_kernel
):
    length = queries.shape[0]
    head_count = saved_state.shape[1]
    columns = head_count * DV
    tap_count = conv_kernel.shape[0]
    query_c = to_heads(queries, head_count, DK)
    key_c = to_heads(key_rows, head_count, DK)
    value_c = to_heads(values, head_count, DV)
    gate_c = to_heads(log_gates, head_count, DK)
    grad_c = to_heads(grad_output, head_count, DV)
    within = jnp.cumsum(gate_c, axis=2)
    running_totals = within[:, :, -1]
    query_up = query_c * jnp.exp(within)
    key_down = key_c * jnp.exp(-within)
    tail = jnp.exp(running_totals[:, :, None] - within)
    key_tail = key_c * tail
    growth = jnp.einsum("hnta,hnte->hnae", key_tail, value_c, precision=PRECISE)
    pushes = jnp.einsum("hnta,hnte->hnae", query_up, grad_c, precision=PRECISE)
    last_state, starts = linked_sequence(running_totals, growth, saved_state[0], False)
    zero_state = jnp.zeros((head_count, DK, DV), jnp.float32)
    shard_push, ends_alone = linked_sequence(running_totals, pushes, zero_state, True)
    all_decay = jnp.sum(running_totals, axis=1)
    shard_decay = jnp.exp(all_decay)
    prefix = prefix_2(
        (shard_decay, shard_push),
        "seq",
        compose,
        (jnp.ones_like(shard_decay), jnp.zeros_like(shard_push)),
    )
    incoming = prefix[1]
    leaving, ends = linked_sequence(running_totals, pushes, incoming, True)
    grad_query, grad_key, grad_value = local_grads(
        grad_c, value_c, within, running_totals, query_up, key_down, key_tail, starts, ends
    )
    terms = query_c * grad_query - key_c * grad_key
    steps_idx = jnp.arange(STRETCH)
    upper_mask = (steps_idx[:, None] <= steps_idx[None, :]).astype(jnp.float32)
    inside = jnp.einsum("ts,hnsa->hnta", upper_mask, terms, precision=PRECISE)
    stretch_sums = jnp.sum(terms, axis=2)
    after = jnp.sum(stretch_sums, axis=1)[:, None] - jnp.cumsum(stretch_sums, axis=1)
    own_term = jnp.sum(incoming * last_state, axis=-1)
    grad_gate = inside + after[:, :, None] + own_term[:, None, None]
    grad_rows = from_heads(grad_value).astype(jnp.bfloat16)
    kernel_part = lax.dynamic_slice_in_dim(
        conv_kernel, lax.axis_index("head") * columns, columns, 1
    )
    next_rows = passed_along(grad_rows[: tap_count - 1], "seq", -1)
    padded = jnp.concatenate([grad_rows, next_rows], axis=0).astype(jnp.float32)
    input_f = conv_input.astype(jnp.float32)
    conv_grad = jnp.zeros((length, columns), jnp.float32)
    tap_terms = []
    for tap_index in range(tap_count):
        window = padded[tap_index : tap_index + length]
        conv_grad = conv_grad + kernel_part[tap_index] * window
        tap_terms.append(jnp.sum(input_f * window, axis=0))
    grad_kernel = lax.psum(jnp.stack(tap_terms), "seq")
    grad_input = lax.all_to_all(
        conv_grad.astype(jnp.bfloat16), "head", split_axis=0, concat_axis=1, tiled=True
    )
    grad_queries = from_heads(grad_query).astype(jnp.bfloat16)
    grad_keys = from_heads(grad_key).astype(jnp.bfloat16)
    grad_gates = from_heads(grad_gate).astype(jnp.bfloat16)
    return (grad_queries, grad_keys, grad_gates, grad_input, grad_kernel)


def solution(mesh):
    placed = (
        P("seq", "head"),
        P("seq", "head"),
        P("seq", "head"),
        P("seq", "head"),
        P("seq", "head"),
        P("seq", "head"),
        P("seq", "head", None, None),
        P(),
    )
    return jax.shard_map(
        per_device,
        mesh=mesh,
        in_specs=placed,
        out_specs=(
            P("seq", "head"),
            P("seq", "head"),
            P("seq", "head"),
            P(("seq", "head"), None),
            P(None, "head"),
        ),
        check_vma=False,
    )
```

profile of v0, /device:TPU:2, one launch (start us, length us, event | category | flops | bytes accessed | tf_op | source)
XLA Modules:
  0.0 805.4 jit_solution(9202336515990108877)
XLA Ops:
  17.8 215.5 %all-gather.2 = f32[128,3,128]{2,1,0:T(4,128)S(1)} all-gather(f32[1,3,128]{2,1,0:T(4,128)S(1)} %exponential_bitcast_fusion.3), channel_id=2, replica_groups=mesh['seq'=128,'head'=8] {'seq'}, dimensions={0}, use_global_device_ids=true | all-gather | bytes 198144 | tf_op jit(solution)/shard_map/all_gather | solution.py:16
  236.5 118.9 %all-gather.5.cloned.1.call-done = f32[384,128,128]{2,1,0:T(8,128)} async-done(((f32[3,128,128]{2,1,0:T(8,128)}), f32[384,128,128]{2,1,0:T(8,128)}) %all-gather.5.cloned.1.call-update) | async-done | bytes 25165840 | tf_op jit(solution)/shard_map/all_gather | solution.py:16
  355.4 146.7 %while.62 = (s32[]{:T(128)}, f32[3,128,128]{2,1,0:T(8,128)S(1)}, s32[]{:T(128)}, f32[128,3,128]{2,1,0:T(4,128)S(1)}, f32[128,3,128,128]{3,2,1,0:T(8,128)}, /*index=5*/s32[]{:T(128)}, s32[]{:T(128)}, s32[]{:T(128)}, s32[]{:T(128)}) while((s32[]{:T(128)}, f32[3,128,128]{2,1,0:T(8,128)S(1)}, s32[]{:T(128)}, ...), condition=%wide.region_7.8_spmd.clone, body=%wide.region_6.7_spmd.clone.sunk | while | flops 196616 | bytes 594599 | solution.py:27
  356.6 1.1 fusion.41
  357.7 1.1 fusion.41
  363.5 1.1 fusion.41
  364.6 1.1 fusion.41
  365.8 1.1 fusion.41
  366.9 1.1 fusion.41
  368.1 1.1 fusion.41
  373.8 1.1 fusion.41
  374.9 1.1 fusion.41
  376.1 1.1 fusion.41
  377.2 1.1 fusion.41
  378.4 1.1 fusion.41
  379.5 1.1 fusion.41
  385.3 1.1 fusion.41
  386.4 1.1 fusion.41
  387.6 1.1 fusion.41
  388.7 1.1 fusion.41
  389.8 1.1 fusion.41
  395.6 1.1 fusion.41
  396.7 1.1 fusion.41
  397.9 1.1 fusion.41
  399.0 1.1 fusion.41
  400.2 1.1 fusion.41
  401.3 1.1 fusion.41
  407.1 1.1 fusion.41
  503.3 1.3 collective-permute-start
  508.3 1.6 collective-permute-done
  511.3 4.9 all-to-all-start
  516.2 281.7 %psum.7 = f32[4,384]{1,0:T(4,128)} all-reduce(f32[4,384]{1,0:T(4,128)S(1)} %pad_maximum_fusion), channel_id=1, replica_groups=mesh['seq'=128,'head'=8] {'seq'}, use_global_device_ids=true, to_apply=%region_18.19 | all-reduce | flops 1536 | bytes 12288 | tf_op jit(solution)/shard_map/psum | solution.py:149
  (313 shorter events, 135.0 us)
Async XLA Ops:
  7.2 348.3 %all-gather.5.cloned.1.call-start = ((), (), s32[]{:S(2)}) async-start(), calls=%async_computation.1 | async-start | bytes 25362432 | tf_op jit(solution)/shard_map/all_gather | solution.py:16
  12.8 0.7 copy-start
  503.3 6.5 collective-permute-start
  511.3 286.6 %all-to-all-start = ((bf16[8,16,384]{2,1,0:T(8,128)(2,1)}), bf16[8,16,384]{2,1,0:T(8,128)(2,1)S(1)}, u32[]{:S(2)}, u32[]{:S(2)}) async-start(bf16[8,16,384]{2,1,0:T(8,128)(2,1)} %bitcast.49), calls=%async_computation | async-start | bytes 196608 | tf_op jit(solution)/shard_map/all_to_all | solution.py:150
Sparse Core Ops, SparseCore 0:
  13.6 341.7 all-gather.4
where the time goes:
time: 809 us; the launch traced here: 805 us
  blocking collectives  497 us (61%)
  other arithmetic  142 us (18%)
  waiting for transfers between devices  121 us (15%)
  local copies, waits for them, and re-layouts  14.7 us (2%)
  between operations  14.4 us (2%)
    psum x1, blocking collectives, per_device(): grad_kernel = lax.psum(jnp.stack(tap_terms), 'seq')  282 us
    all_gather x1, blocking collectives, prefix_2(): everything = jax.tree.map(lambda part: lax.all_gather(part, axis), x)  215 us
    select_n x128, other arithmetic, hop(): return jax.tree.map(lambda a, b: jnp.where(reached, a, b), new, before)  140 us
    all_gather x1, waiting for transfers between devices, prefix_2(): everything = jax.tree.map(lambda part: lax.all_gather(part, axis), x)  119 us
  transfers between devices with their start and end apart: 3, of which 2 were waited for; matrix products, arithmetic and copies ran while one was open for 1% of the time, Pallas kernels for 0%

commit v1 on v0

--- a/solution.py
+++ b/solution.py
@@ -1,7 +1,7 @@
 import jax
 import jax.numpy as jnp
 from jax import lax
-from jax.sharding import PartitionSpec as P
+from jax.sharding import Mesh, PartitionSpec as P
 
 DK = 128
 DV = 128
@@ -11,20 +11,41 @@
 PRECISE = lax.Precision.HIGHEST
 
 
-def prefix_2(x, axis, combine, identity):
-    count, position = (lax.axis_size(axis), lax.axis_index(axis))
-    everything = jax.tree.map(lambda part: lax.all_gather(part, axis), x)
-    start = jax.tree.map(
-        lambda part, zero: jnp.broadcast_to(jnp.asarray(zero, part.dtype), part.shape), x, identity
-    )
+SEQ = ("y", "zh", "zl")
+HEAD = ("x", "core")
 
-    def hop(k, before):
-        at = count - 1 - k
-        reached = at > position
-        new = combine(before, jax.tree.map(lambda part: part[at], everything))
-        return jax.tree.map(lambda a, b: jnp.where(reached, a, b), new, before)
 
-    return lax.fori_loop(0, count, hop, start)
+def exchange(x, axis):
+    return lax.all_to_all(x, axis, 0, 0, tiled=True)
+
+
+def later_blocks(log_decay, push):
+    head_count, dk, dv = push.shape
+    count = lax.axis_size(SEQ)
+    rows = head_count * dk // count
+    logs = log_decay.reshape(count, rows)
+    high = lax.reduce_precision(logs, 8, 7)
+    low = logs - high
+    tail = jnp.concatenate([high, low], axis=1)
+    tail = jnp.pad(tail, ((0, 0), (0, dv - 2 * rows)))[:, None]
+    sent = jnp.concatenate([push.reshape(count, rows, dv), tail], axis=1).astype(jnp.bfloat16)
+    got = exchange(sent, SEQ).astype(jnp.float32)
+    logs = (got[:, rows, :rows] + got[:, rows, rows : 2 * rows]).T
+    at = jnp.arange(count)
+    totals = jnp.einsum("rb,bc->rc", logs, (at[:, None] <= at[None, :]).astype(jnp.float32), precision=PRECISE)
+    before = totals - logs
+    gap = before[:, None, :] - totals[:, :, None]
+    weight = jnp.where(at[:, None] < at[None, :], jnp.exp(jnp.minimum(gap, 0.0)), 0.0)
+    ended = jnp.einsum("rbc,cre->bre", weight, got[:, :rows], precision=PRECISE)
+    back = exchange(ended.astype(jnp.bfloat16), SEQ)
+    return back.astype(jnp.float32).reshape(head_count, dk, dv)
+
+
+def sum_all(x):
+    for axis in (("y", "zl"), "zh"):
+        every = jnp.broadcast_to(x[None], (lax.axis_size(axis),) + x.shape)
+        x = jnp.sum(exchange(every, axis), axis=0)
+    return x
 
 
 def passed_along(x, axis, by):
@@ -85,10 +106,6 @@
     return (grad_query, grad_key, grad_value)
 
 
-def compose(earlier, later):
-    return (earlier[0] * later[0], later[0][..., None] * earlier[1] + later[1])
-
-
 def per_device(
     queries, key_rows, values, conv_input, log_gates, grad_output, saved_state, conv_kernel
 ):
@@ -113,14 +130,7 @@
     zero_state = jnp.zeros((head_count, DK, DV), jnp.float32)
     shard_push, ends_alone = linked_sequence(running_totals, pushes, zero_state, True)
     all_decay = jnp.sum(running_totals, axis=1)
-    shard_decay = jnp.exp(all_decay)
-    prefix = prefix_2(
-        (shard_decay, shard_push),
-        "seq",
-        compose,
-        (jnp.ones_like(shard_decay), jnp.zeros_like(shard_push)),
-    )
-    incoming = prefix[1]
+    incoming = later_blocks(all_decay, shard_push)
     leaving, ends = linked_sequence(running_totals, pushes, incoming, True)
     grad_query, grad_key, grad_value = local_grads(
         grad_c, value_c, within, running_totals, query_up, key_down, key_tail, starts, ends
@@ -135,20 +145,22 @@
     grad_gate = inside + after[:, :, None] + own_term[:, None, None]
     grad_rows = from_heads(grad_value).astype(jnp.bfloat16)
     kernel_part = lax.dynamic_slice_in_dim(
-        conv_kernel, lax.axis_index("head") * columns, columns, 1
+        conv_kernel, lax.axis_index(HEAD) * columns, columns, 1
     )
-    next_rows = passed_along(grad_rows[: tap_count - 1], "seq", -1)
+    before_rows = passed_along(conv_input[1 - tap_count :], SEQ, 1)
+    input_f = jnp.concatenate([before_rows, conv_input], axis=0).astype(jnp.float32)
+    next_rows = passed_along(grad_rows[: tap_count - 1], SEQ, -1)
     padded = jnp.concatenate([grad_rows, next_rows], axis=0).astype(jnp.float32)
-    input_f = conv_input.astype(jnp.float32)
+    own_rows = grad_rows.astype(jnp.float32)
     conv_grad = jnp.zeros((length, columns), jnp.float32)
     tap_terms = []
     for tap_index in range(tap_count):
-        window = padded[tap_index : tap_index + length]
-        conv_grad = conv_grad + kernel_part[tap_index] * window
-        tap_terms.append(jnp.sum(input_f * window, axis=0))
-    grad_kernel = lax.psum(jnp.stack(tap_terms), "seq")
+        conv_grad = conv_grad + kernel_part[tap_index] * padded[tap_index : tap_index + length]
+        start = tap_count - 1 - tap_index
+        tap_terms.append(jnp.sum(input_f[start : start + length] * own_rows, axis=0))
+    grad_kernel = sum_all(jnp.stack(tap_terms))
     grad_input = lax.all_to_all(
-        conv_grad.astype(jnp.bfloat16), "head", split_axis=0, concat_axis=1, tiled=True
+        conv_grad.astype(jnp.bfloat16), HEAD, split_axis=0, concat_axis=1, tiled=True
     )
     grad_queries = from_heads(grad_query).astype(jnp.bfloat16)
     grad_keys = from_heads(grad_key).astype(jnp.bfloat16)
@@ -157,26 +169,12 @@
 
 
 def solution(mesh):
-    placed = (
-        P("seq", "head"),
-        P("seq", "head"),
-        P("seq", "head"),
-        P("seq", "head"),
-        P("seq", "head"),
-        P("seq", "head"),
-        P("seq", "head", None, None),
-        P(),
-    )
+    fine = Mesh(mesh.devices.reshape(4, 8, 4, 4, 2), SEQ + HEAD)
+    rows = P(SEQ, HEAD)
     return jax.shard_map(
         per_device,
-        mesh=mesh,
-        in_specs=placed,
-        out_specs=(
-            P("seq", "head"),
-            P("seq", "head"),
-            P("seq", "head"),
-            P(("seq", "head"), None),
-            P(None, "head"),
-        ),
+        mesh=fine,
+        in_specs=(rows, rows, rows, rows, rows, rows, P(SEQ, HEAD, None, None), P()),
+        out_specs=(rows, rows, rows, P(SEQ + HEAD, None), P(None, HEAD)),
         check_vma=False,
     )

time: 809 us -> 168 us (0.21)
  the two profiles are of different devices: /device:TPU:2 before, /device:TPU:8 now
where the time goes in v1:
time: 168 us; the launch traced here: 167 us
  waiting for transfers between devices  81.5 us (49%)
  starting transfers between devices  61.6 us (37%)
  local copies, waits for them, and re-layouts  13.7 us (8%)
  matrix products  5.07 us (3%)
  other arithmetic  3.85 us (2%)
    all_to_all x4, waiting for transfers between devices, exchange(): return lax.all_to_all(x, axis, 0, 0, tiled=True)  73.6 us
    all_to_all x4, starting transfers between devices, exchange(): return lax.all_to_all(x, axis, 0, 0, tiled=True)  50.1 us
    ppermute x2, starting transfers between devices, passed_along(): return lax.ppermute(x, axis, pairs)  7.19 us
    unnamed x25, local copies, waits for them, and re-layouts  7.08 us
    all_to_all x1, waiting for transfers between devices, per_device(): lax.all_to_all(conv_grad.astype(jnp.bfloat16), HEAD, split_axis=0, concat...  5.76 us
    all_to_all x1, starting transfers between devices, per_device(): lax.all_to_all(conv_grad.astype(jnp.bfloat16), HEAD, split_axis=0, concat...  4.29 us
  transfers between devices with their start and end apart: 7, of which 5 were waited for; matrix products, arithmetic and copies ran while one was open for 7% of the time, Pallas kernels for 0%

profile of v1, /device:TPU:8, one launch (start us, length us, event | category | flops | bytes accessed | tf_op | source)
XLA Modules:
  0.0 166.9 jit_solution(18432656594315725847)
XLA Ops:
  0.7 0.9 copy-done.2
  1.8 0.8 copy-done.3
  2.9 0.8 copy-done.4
  4.1 0.5 convolution_bitcast_fusion
  5.5 0.8 pad_maximum_fusion
  6.3 33.0 %all-to-all-start = ((bf16[128,4,128]{2,1,0:T(4,128)(2,1)}), bf16[128,4,128]{2,1,0:T(4,128)(2,1)S(1)}, u32[]{:S(2)}, u32[]{:S(2)}) async-start(bf16[128,4,128]{2,1,0:T(4,128)(2,1)} %pad_maximum_fusion), calls=%async_computation | async-start | bytes 262144 | tf_op jit(solution)/shard_map/all_to_all | solution.py:19
  39.5 3.4 %collective-permute-start.1 = (bf16[3,384]{0,1:T(8,128)(2,1)S(1)}, bf16[3,384]{0,1:T(8,128)(2,1)S(1)}, u32[]{:S(2)}, u32[]{:S(2)}) collective-permute-start(bf16[3,384]{0,1:T(8,128)(2,1)S(1)} %copy.353), channel_id=1, source_target_pairs={{0,8},{8,16},{16,24},{24,32},{32,40},{40,48},{48,56},{56,64},{64,7... | collective-permute-start | bytes 6920 | tf_op jit(solution)/shard_map/ppermute | solution.py:54
  43.3 0.8 copy-done.6
  44.5 0.5 convolution_bitcast_fusion.1
  45.0 0.9 copy-done
  46.3 0.5 convolution_bitcast_fusion.3
  46.8 24.3 %all-to-all-done = bf16[128,4,128]{2,1,0:T(4,128)(2,1)S(1)} async-done(((bf16[128,4,128]{2,1,0:T(4,128)(2,1)}), bf16[128,4,128]{2,1,0:T(4,128)(2,1)S(1)}, u32[]{:S(2)}, u32[]{:S(2)}) %all-to-all-start) | async-done | bytes 131104 | tf_op jit(solution)/shard_map/all_to_all | solution.py:19
  71.9 0.8 copy.343
  72.7 7.0 %all-to-all-start.1 = ((bf16[128,3,128]{2,1,0:T(4,128)(2,1)}), bf16[128,3,128]{2,1,0:T(4,128)(2,1)S(1)}, u32[]{:S(2)}, u32[]{:S(2)}) async-start(bf16[128,3,128]{2,1,0:T(4,128)(2,1)} %copy.343), calls=%async_computation.1 | async-start | bytes 262144 | tf_op jit(solution)/shard_map/all_to_all | solution.py:19
  81.0 28.9 %all-to-all-done.1 = bf16[128,3,128]{2,1,0:T(4,128)(2,1)S(1)} async-done(((bf16[128,3,128]{2,1,0:T(4,128)(2,1)}), bf16[128,3,128]{2,1,0:T(4,128)(2,1)S(1)}, u32[]{:S(2)}, u32[]{:S(2)}) %all-to-all-start.1) | async-done | bytes 98336 | tf_op jit(solution)/shard_map/all_to_all | solution.py:19
  111.6 0.7 broadcast_in_dim.31
  112.2 5.1 %all-to-all-start.3 = ((f32[16,4,384]{2,1,0:T(4,128)}), f32[16,4,384]{2,1,0:T(4,128)S(1)}, u32[]{:S(2)}, u32[]{:S(2)}) async-start(f32[16,4,384]{2,1,0:T(4,128)} %broadcast_in_dim.31), calls=%async_computation.3 | async-start | bytes 196608 | tf_op jit(solution)/shard_map/all_to_all | solution.py:19
  117.8 0.9 dynamic-slice_reduce_fusion.3
  118.7 3.8 %collective-permute-start = (bf16[3,384]{0,1:T(8,128)(2,1)S(1)}, bf16[3,384]{0,1:T(8,128)(2,1)S(1)}, u32[]{:S(2)}, u32[]{:S(2)}) collective-permute-start(bf16[3,384]{0,1:T(8,128)(2,1)S(1)} %bitcast.158), channel_id=1, source_target_pairs={{8,0},{16,8},{24,16},{32,24},{40,32},{48,40},{56,48},{64,56},{72,6... | collective-permute-start | bytes 6920 | tf_op jit(solution)/shard_map/ppermute | solution.py:54
  122.6 0.6 fusion.44
  123.2 2.1 %collective-permute-done = bf16[3,384]{0,1:T(8,128)(2,1)S(1)} collective-permute-done((bf16[3,384]{0,1:T(8,128)(2,1)S(1)}, bf16[3,384]{0,1:T(8,128)(2,1)S(1)}, u32[]{:S(2)}, u32[]{:S(2)}) %collective-permute-start) | collective-permute-done | bytes 2336 | tf_op jit(solution)/shard_map/ppermute | solution.py:54
  125.7 0.8 copy.351
  126.5 4.3 %all-to-all-start.2 = ((bf16[8,16,384]{2,1,0:T(8,128)(2,1)}), bf16[8,16,384]{2,1,0:T(8,128)(2,1)S(1)}, u32[]{:S(2)}, u32[]{:S(2)}) async-start(bf16[8,16,384]{2,1,0:T(8,128)(2,1)} %bitcast.51), calls=%async_computation.2 | async-start | bytes 196608 | tf_op jit(solution)/shard_map/all_to_all | solution.py:162
  130.8 5.8 %all-to-all-done.2 = bf16[8,16,384]{2,1,0:T(8,128)(2,1)S(1)} async-done(((bf16[8,16,384]{2,1,0:T(8,128)(2,1)}), bf16[8,16,384]{2,1,0:T(8,128)(2,1)S(1)}, u32[]{:S(2)}, u32[]{:S(2)}) %all-to-all-start.2) | async-done | bytes 98336 | tf_op jit(solution)/shard_map/all_to_all | solution.py:162
  136.6 0.6 broadcast_in_dim.32
  137.2 5.0 %all-to-all-start.4 = ((f32[8,4,384]{2,1,0:T(4,128)}), f32[8,4,384]{2,1,0:T(4,128)S(1)}, u32[]{:S(2)}, u32[]{:S(2)}) async-start(f32[8,4,384]{2,1,0:T(4,128)} %broadcast_in_dim.32), calls=%async_computation.4 | async-start | bytes 98304 | tf_op jit(solution)/shard_map/all_to_all | solution.py:19
  142.7 0.8 copy.359
  143.6 0.8 copy.357
  144.5 0.8 copy.358
  145.3 0.7 copy.367
  145.9 20.4 %all-to-all-done.4 = f32[8,4,384]{2,1,0:T(4,128)S(1)} async-done(((f32[8,4,384]{2,1,0:T(4,128)}), f32[8,4,384]{2,1,0:T(4,128)S(1)}, u32[]{:S(2)}, u32[]{:S(2)}) %all-to-all-start.4) | async-done | bytes 49184 | tf_op jit(solution)/shard_map/all_to_all | solution.py:19
  166.3 0.6 reduce_sum.99
  (93 shorter events, 9.6 us)
Async XLA Ops:
  0.6 0.9 copy-start.2
  1.7 0.9 copy-start.3
  2.7 0.9 copy-start.4
  6.3 33.0 %copy-start.1 = (bf16[128,384]{1,0:T(8,128)(2,1)S(1)}, bf16[128,384]{1,0:T(8,128)(2,1)}, u32[]{:S(2)}) copy-start(bf16[128,384]{1,0:T(8,128)(2,1)} %param.17) | copy-start | bytes 294916
  6.3 64.8 %all-to-all-start = ((bf16[128,4,128]{2,1,0:T(4,128)(2,1)}), bf16[128,4,128]{2,1,0:T(4,128)(2,1)S(1)}, u32[]{:S(2)}, u32[]{:S(2)}) async-start(bf16[128,4,128]{2,1,0:T(4,128)(2,1)} %pad_maximum_fusion), calls=%async_computation | async-start | bytes 262144 | tf_op jit(solution)/shard_map/all_to_all | solution.py:19
  39.3 3.6 %copy-start.5 = (bf16[128,384]{1,0:T(8,128)(2,1)S(1)}, bf16[128,384]{1,0:T(8,128)(2,1)}, u32[]{:S(2)}) copy-start(bf16[128,384]{1,0:T(8,128)(2,1)} %param.15) | copy-start | bytes 294916
  39.5 41.3 %collective-permute-start.1 = (bf16[3,384]{0,1:T(8,128)(2,1)S(1)}, bf16[3,384]{0,1:T(8,128)(2,1)S(1)}, u32[]{:S(2)}, u32[]{:S(2)}) collective-permute-start(bf16[3,384]{0,1:T(8,128)(2,1)S(1)} %copy.353), channel_id=1, source_target_pairs={{0,8},{8,16},{16,24},{24,32},{32,40},{40,48},{48,56},{56,64},{64,7... | collective-permute-start | bytes 6920 | tf_op jit(solution)/shard_map/ppermute | solution.py:54
  43.1 0.9 copy-start.6
  45.0 0.9 copy-start
  72.7 37.2 %all-to-all-start.1 = ((bf16[128,3,128]{2,1,0:T(4,128)(2,1)}), bf16[128,3,128]{2,1,0:T(4,128)(2,1)S(1)}, u32[]{:S(2)}, u32[]{:S(2)}) async-start(bf16[128,3,128]{2,1,0:T(4,128)(2,1)} %copy.343), calls=%async_computation.1 | async-start | bytes 262144 | tf_op jit(solution)/shard_map/all_to_all | solution.py:19
  112.2 14.2 %all-to-all-start.3 = ((f32[16,4,384]{2,1,0:T(4,128)}), f32[16,4,384]{2,1,0:T(4,128)S(1)}, u32[]{:S(2)}, u32[]{:S(2)}) async-start(f32[16,4,384]{2,1,0:T(4,128)} %broadcast_in_dim.31), calls=%async_computation.3 | async-start | bytes 196608 | tf_op jit(solution)/shard_map/all_to_all | solution.py:19
  118.7 6.5 %collective-permute-start = (bf16[3,384]{0,1:T(8,128)(2,1)S(1)}, bf16[3,384]{0,1:T(8,128)(2,1)S(1)}, u32[]{:S(2)}, u32[]{:S(2)}) collective-permute-start(bf16[3,384]{0,1:T(8,128)(2,1)S(1)} %bitcast.158), channel_id=1, source_target_pairs={{8,0},{16,8},{24,16},{32,24},{40,32},{48,40},{56,48},{64,56},{72,6... | collective-permute-start | bytes 6920 | tf_op jit(solution)/shard_map/ppermute | solution.py:54
  126.5 10.1 %all-to-all-start.2 = ((bf16[8,16,384]{2,1,0:T(8,128)(2,1)}), bf16[8,16,384]{2,1,0:T(8,128)(2,1)S(1)}, u32[]{:S(2)}, u32[]{:S(2)}) async-start(bf16[8,16,384]{2,1,0:T(8,128)(2,1)} %bitcast.51), calls=%async_computation.2 | async-start | bytes 196608 | tf_op jit(solution)/shard_map/all_to_all | solution.py:162
  137.2 29.1 %all-to-all-start.4 = ((f32[8,4,384]{2,1,0:T(4,128)}), f32[8,4,384]{2,1,0:T(4,128)S(1)}, u32[]{:S(2)}, u32[]{:S(2)}) async-start(f32[8,4,384]{2,1,0:T(4,128)} %broadcast_in_dim.32), calls=%async_computation.4 | async-start | bytes 98304 | tf_op jit(solution)/shard_map/all_to_all | solution.py:19

commit v2 on v1

v2 whole, which is shorter than its diff:
```python
import jax
import jax.numpy as jnp
from jax import lax
from jax.experimental import pallas as pl
from jax.experimental.pallas import tpu as pltpu
from jax.sharding import Mesh, PartitionSpec as P

HEADS = 3
WIDTH = 128
LEN = 128
STRETCH = 64
TAPS = 4
NEAR = 16
FAR = 8
PEERS = 8
ROWS = 32
SEQ = ("y", "zh", "zl")
HEAD = ("x", "core")
GROUP = ("y", "zl")
F32 = jnp.float32
BF16 = jnp.bfloat16
PRECISE = lax.Precision.HIGHEST


def dot(a, b, over_a=1, over_b=0, precision=None):
    return lax.dot_general(
        a, b, (((over_a,), (over_b,)), ((), ())), precision=precision, preferred_element_type=F32
    )


def dot_exact(a, b, over_a=1, over_b=0):
    return dot(a.astype(F32), b.astype(F32), over_a, over_b, PRECISE)


def two_parts(a):
    high = a.astype(BF16)
    return high, (a - high.astype(F32)).astype(BF16)


def dot_left(a, b, over_a=1, over_b=0):
    high, low = two_parts(a)
    return dot(high, b, over_a, over_b) + dot(low, b, over_a, over_b)


def dot_right(a, b, over_a=1, over_b=0):
    high, low = two_parts(b)
    return dot(a, high, over_a, over_b) + dot(a, low, over_a, over_b)


def ordered(size, compare):
    row = lax.broadcasted_iota(jnp.int32, (size, size), 0)
    column = lax.broadcasted_iota(jnp.int32, (size, size), 1)
    return compare(row, column)


def head_of(x, h):
    return x[:, h * WIDTH : (h + 1) * WIDTH]


def tail_rows(logs):
    row = lax.broadcasted_iota(jnp.int32, (8, WIDTH), 0)
    tail = jnp.zeros((8, WIDTH), F32)
    for h in range(HEADS):
        high = logs[h].astype(BF16).astype(F32)
        low = logs[h] - high
        tail = jnp.where(row == h, high, tail)
        tail = jnp.where(row == HEADS + h, low, tail)
    return tail


def push_of(queries, log_gates, grad_output):
    lower = ordered(LEN, lambda r, c: r >= c).astype(F32).astype(BF16)
    within = dot(lower, log_gates)
    query_up = queries.astype(F32) * jnp.exp(within)
    pushes = [
        dot_left(head_of(query_up, h), head_of(grad_output, h), 0, 0).reshape(NEAR, 8, WIDTH)
        for h in range(HEADS)
    ]
    last = within[LEN - 1 : LEN]
    tail = tail_rows([head_of(last, h) for h in range(HEADS)])
    tail = jnp.broadcast_to(tail[None], (NEAR, 8, WIDTH))
    return jnp.concatenate(pushes + [tail], axis=1).astype(BF16)


def logs_of(tail):
    return [tail[h : h + 1] + tail[HEADS + h : HEADS + h + 1] for h in range(HEADS)]


def decays_of(logs, place):
    lane = lax.broadcasted_iota(jnp.int32, (8, WIDTH), 1)
    row = lax.broadcasted_iota(jnp.int32, (8, WIDTH), 0)
    mine = lane == row + 8 * place
    picked = [jnp.sum(jnp.where(mine, logs[h], 0.0), axis=1, keepdims=True) for h in range(HEADS)]
    return jnp.concatenate([jnp.broadcast_to(jnp.exp(p), (8, WIDTH)) for p in picked], axis=0)


def run_of(got, place):
    x = got.astype(F32)
    logs = logs_of(x[8 * HEADS :])
    return x[: 8 * HEADS], decays_of(logs, place), logs


def group_of(got, place):
    runs = []
    for y in range(4):
        running = jnp.zeros((8 * HEADS, WIDTH), F32)
        total = [jnp.zeros((1, WIDTH), F32)] * HEADS
        for zl in (3, 2, 1, 0):
            push, decay, logs = run_of(got[y * 4 + zl], place)
            running = push + decay * running
            total = [a + b for a, b in zip(total, logs)]
        runs.append(jnp.concatenate([running, tail_rows(total)], axis=0).astype(BF16))
    return runs


def ends_of(near, far, place, mine):
    ends = [None] * NEAR
    running = jnp.zeros((8 * HEADS, WIDTH), F32)
    for y in (3, 2, 1, 0):
        entering = jnp.zeros((8 * HEADS, WIDTH), F32)
        for zh in range(FAR - 1, -1, -1):
            entering = jnp.where(mine == zh, running, entering)
            push, decay, _ = run_of(far[zh, y], place)
            running = push + decay * running
        for zl in (3, 2, 1, 0):
            ends[y * 4 + zl] = entering.astype(BF16)
            push, decay, _ = run_of(near[y * 4 + zl], place)
            entering = push + decay * entering
    return ends


def local_of(queries, key_rows, values, log_gates, grad_output, start):
    q, k = queries.astype(F32), key_rows.astype(F32)
    lower = ordered(STRETCH, lambda r, c: r >= c)
    stretches = []
    for n in (0, 1):
        part = slice(n * STRETCH, (n + 1) * STRETCH)
        within = dot(lower.astype(F32).astype(BF16), log_gates[part])
        total = within[STRETCH - 1 : STRETCH]
        column = dot_exact(
            log_gates[part], jnp.ones((STRETCH, WIDTH), F32), 0, 0
        )
        stretches.append((part, within, total, jnp.exp(column)))
    states, pushes, tails = [start], [], []
    for part, within, total, decay in stretches:
        tail = jnp.exp(total - within)
        tails.append(tail)
        growth = dot_exact(k[part] * tail, values[part], 0, 0)
        states.append(decay * states[-1] + growth)
        pushes.append(dot_exact(q[part] * jnp.exp(within), grad_output[part], 0, 0))
    ends = [pushes[1], None]
    grad_q, grad_k, grad_v = [], [], []
    for n, (part, within, total, decay) in enumerate(stretches):
        up, down = jnp.exp(within), jnp.exp(-within)
        query_up, key_down = q[part] * up, k[part] * down
        go, v = grad_output[part], values[part]
        scores = jnp.where(lower, dot(go, v, 1, 1), 0.0)
        grad_q.append(up * (dot_exact(go, states[n], 1, 1) + dot_exact(scores, key_down)))
        grad = down * dot_exact(scores, query_up, 0, 0)
        weights = jnp.where(lower, dot_exact(query_up, key_down, 1, 1), 0.0)
        grad_value = dot_exact(weights, go, 0, 0)
        if ends[n] is not None:
            grad = grad + tails[n] * dot_exact(v, ends[n], 1, 1)
            grad_value = grad_value + dot_exact(k[part] * tails[n], ends[n])
        grad_k.append(grad)
        grad_v.append(grad_value)
    grad_q, grad_k = jnp.concatenate(grad_q, axis=0), jnp.concatenate(grad_k, axis=0)
    upper = ordered(LEN, lambda r, c: r <= c).astype(F32)
    gate = dot_exact(upper, q * grad_q - k * grad_k)
    tail = jnp.concatenate([tails[0] * jnp.exp(stretches[1][2]), tails[1]], axis=0)
    return grad_q.astype(BF16), grad_k, jnp.concatenate(grad_v, axis=0), gate, tail, states[2]


def final_of(end, values, key_rows, tail, grad_k, grad_v, gate, last):
    added = tail * dot(values, end, 1, 1)
    k = key_rows.astype(F32)
    grad_value = grad_v + dot_left(k * tail, end)
    upper = ordered(LEN, lambda r, c: r <= c).astype(F32).astype(BF16)
    own = dot_right(jnp.ones((8, WIDTH), BF16), end.astype(F32) * last, 1, 1)[:1]
    gate = gate - dot_right(upper, k * added) + own
    return (grad_k + added).astype(BF16), grad_value.astype(BF16), gate.astype(BF16)


def push_kernel(queries, log_gates, grad_output, out):
    out[...] = push_of(queries[...], log_gates[...], grad_output[...])


def group_kernel(place, got, out):
    runs = group_of(got, place[0])
    for y in range(4):
        for zh in range(FAR):
            out[zh, y] = runs[y]


def ends_kernel(place, near, far, out):
    ends = ends_of(near, far, place[0], place[1])
    for i in range(NEAR):
        out[i] = ends[i]


def local_kernel(queries, key_rows, values, log_gates, grad_output, start, grad_q, grad_k, grad_v, gate, tail, last):
    for h in range(HEADS):
        at = slice(h * WIDTH, (h + 1) * WIDTH)
        results = local_of(
            queries[:, at], key_rows[:, at], values[:, at], log_gates[:, at], grad_output[:, at], start[0, h]
        )
        for ref, value in zip((grad_q, grad_k, grad_v, gate, tail), results):
            ref[:, at] = value
        last[h] = results[5]


def final_kernel(
    ends, values, key_rows, tail, grad_k, grad_v, gate, last, inputs, before, out_k, out_gate, out_v, taps, padded
):
    padded[:8] = before[...].astype(F32)
    padded[8:] = inputs[...].astype(F32)
    every = ends[...].astype(F32)
    for h in range(HEADS):
        at = slice(h * WIDTH, (h + 1) * WIDTH)
        end = every[:, 8 * h : 8 * h + 8].reshape(LEN, WIDTH).astype(BF16)
        grad_key, grad_value, grad_gate = final_of(
            end, values[:, at], key_rows[:, at], tail[:, at], grad_k[:, at], grad_v[:, at], gate[:, at], last[h]
        )
        out_k[:, at] = grad_key
        out_v[:, at] = grad_value
        out_gate[:, at] = grad_gate
        rounded = grad_value.astype(F32)
        for tap in range(TAPS):
            term = jnp.sum(padded[8 - tap : 8 - tap + LEN, at] * rounded, axis=0, keepdims=True)
            taps[:, tap : tap + 1, at] = jnp.broadcast_to(term[None], (NEAR, 1, WIDTH))


def conv_kernel_body(place, grad_v, after, weights, *outs):
    outs, padded, rows = outs[:PEERS], outs[PEERS], outs[PEERS + 1]
    padded[:LEN] = grad_v[...].astype(F32)
    padded[LEN:] = after[...].astype(F32)
    total = weights[0:1] * padded[0:LEN]
    for tap in range(1, TAPS):
        total = total + weights[tap : tap + 1] * padded[tap : tap + LEN]
    rows[...] = total.reshape(PEERS, LEN // PEERS, HEADS * WIDTH)
    for r in range(PEERS):
        outs[r][...] = rows[place[2] ^ r].astype(BF16)


def join_kernel(place, *refs):
    out = refs[PEERS]
    for r in range(PEERS):
        start = pl.multiple_of((place[2] ^ r) * (HEADS * WIDTH), WIDTH)
        out[:, pl.ds(start, HEADS * WIDTH)] = refs[r][...]


def spread_kernel(got, out):
    total = jnp.sum(got[...], axis=0)
    out[...] = jnp.broadcast_to(total[None], out.shape)


def total_kernel(got, out):
    out[...] = jnp.sum(got[...], axis=0)


def call(kernel, outs, scalars=0, scratch=()):
    shapes = [jax.ShapeDtypeStruct(shape, dtype) for shape, dtype in outs]
    vmem = pl.BlockSpec()

    def run(*args):
        return pl.pallas_call(
            kernel,
            out_shape=shapes,
            in_specs=[pl.BlockSpec(memory_space=pltpu.SMEM)] * scalars + [vmem] * (len(args) - scalars),
            out_specs=[vmem] * len(outs),
            scratch_shapes=list(scratch),
        )(*args)

    return run


def exchange(x, axis):
    return lax.all_to_all(x, axis, 0, 0, tiled=True)


def passed_along(x, by):
    count = lax.axis_size(SEQ)
    pairs = [(i, i + by) for i in range(count) if 0 <= i + by < count]
    return lax.ppermute(x, SEQ, pairs)


def per_device(queries, key_rows, values, conv_input, log_gates, grad_output, saved_state, conv_kernel):
    columns = HEADS * WIDTH
    wide = (LEN, columns)
    place = jnp.stack([lax.axis_index(GROUP), lax.axis_index("zh"), lax.axis_index(HEAD)]).astype(jnp.int32)
    (sent,) = call(push_kernel, [((NEAR, ROWS, WIDTH), BF16)])(queries, log_gates, grad_output)
    near = exchange(sent, GROUP)
    (sent,) = call(group_kernel, [((FAR, 4, ROWS, WIDTH), BF16)], 1)(place, near)
    far = exchange(sent, "zh")
    locals_ = call(
        local_kernel, [(wide, BF16), (wide, F32), (wide, F32), (wide, F32), (wide, F32), ((HEADS, WIDTH, WIDTH), F32)]
    )(queries, key_rows, values, log_gates, grad_output, saved_state)
    before = passed_along(conv_input[-8:], 1)
    near, before, locals_ = lax.optimization_barrier((near, before, locals_))
    grad_queries, grad_k, grad_v, gate, tail, last = locals_
    (sent,) = call(ends_kernel, [((NEAR, 8 * HEADS, WIDTH), BF16)], 1)(place, near, far)
    ends = exchange(sent, GROUP)
    weights = lax.dynamic_slice_in_dim(conv_kernel, lax.axis_index(HEAD) * columns, columns, 1)
    grad_keys, grad_gates, grad_rows, taps = call(
        final_kernel,
        [(wide, BF16), (wide, BF16), (wide, BF16), ((NEAR, TAPS, columns), F32)],
        scratch=[pltpu.VMEM((LEN + 8, columns), F32)],
    )(ends, values, key_rows, tail, grad_k, grad_v, gate, last, conv_input, before)
    (taps,) = call(spread_kernel, [((FAR, TAPS, columns), F32)])(exchange(taps, GROUP))
    summed = exchange(taps, "zh")
    after = passed_along(grad_rows[:8], -1)
    piece = (LEN // PEERS, columns)
    pieces = call(
        conv_kernel_body,
        [(piece, BF16)] * PEERS,
        1,
        [pltpu.VMEM((LEN + 8, columns), F32), pltpu.VMEM((PEERS,) + piece, F32)],
    )(place, grad_rows, after, weights)
    pieces = list(pieces[:1]) + [
        lax.ppermute(pieces[r], HEAD, [(i, i ^ r) for i in range(PEERS)]) for r in range(1, PEERS)
    ]
    (grad_input,) = call(join_kernel, [((LEN // PEERS, PEERS * columns), BF16)], 1)(place, *pieces)
    (grad_kernel,) = call(total_kernel, [((TAPS, columns), F32)])(summed)
    return (grad_queries, grad_keys, grad_gates, grad_input, grad_kernel)


def solution(mesh):
    fine = Mesh(mesh.devices.reshape(4, FAR, 4, 4, 2), SEQ + HEAD)
    rows = P(SEQ, HEAD)
    return jax.shard_map(
        per_device,
        mesh=fine,
        in_specs=(rows, rows, rows, rows, rows, rows, P(SEQ, HEAD, None, None), P()),
        out_specs=(rows, rows, rows, P(SEQ + HEAD, None), P(None, HEAD)),
        check_vma=False,
    )
```

time: 168 us -> 164 us (0.976)
  the two profiles are of different devices: /device:TPU:8 before, /device:TPU:9 now
where the time goes in v2:
time: 164 us; the launch traced here: 163 us
  starting transfers between devices  73.5 us (45%)
  waiting for transfers between devices  31.8 us (19%)
  blocking collectives  29 us (18%)
  Pallas kernels  21.6 us (13%)
  local copies, waits for them, and re-layouts  5.15 us (3%)
    all_to_all x3, starting transfers between devices, exchange(): return lax.all_to_all(x, axis, 0, 0, tiled=True)  39.7 us
    all_to_all x2, blocking collectives, exchange(): return lax.all_to_all(x, axis, 0, 0, tiled=True)  29 us
    all_to_all x3, waiting for transfers between devices, exchange(): return lax.all_to_all(x, axis, 0, 0, tiled=True)  26.4 us
    ppermute x7, starting transfers between devices, per_device(): lax.ppermute(pieces[r], HEAD, [(i, i ^ r) for i in range(PEERS)])  26.2 us
    pallas_call x9, Pallas kernels, run(): pl.pallas_call(kernel, out_shape=shapes, in_specs=[pl.BlockSpec(memory_sp...  21.6 us
    ppermute x2, starting transfers between devices, passed_along(): return lax.ppermute(x, SEQ, pairs)  7.61 us
    ppermute x7, waiting for transfers between devices, per_device(): lax.ppermute(pieces[r], HEAD, [(i, i ^ r) for i in range(PEERS)])  3.87 us
  transfers between devices with their start and end apart: 12, of which 5 were waited for; matrix products, arithmetic and copies ran while one was open for 2% of the time, Pallas kernels for 6%

profile of v2, /device:TPU:9, one launch (start us, length us, event | category | flops | bytes accessed | tf_op | source)
XLA Modules:
  0.0 162.6 jit_solution(15490156513155754865)
XLA Ops:
  0.6 2.1 %shard_map.119 = bf16[16,32,128]{2,1,0:T(8,128)(2,1)} custom-call(bf16[128,384]{1,0:T(8,128)(2,1)} %queries.3, bf16[128,384]{1,0:T(8,128)(2,1)} %log_gates.3, bf16[128,384]{1,0:T(8,128)(2,1)} %grad_output.3), custom_call_target="tpu_custom_call" | custom-call | tf_op jit(solution)/shard_map/pallas_call | solution.py:266
  2.7 8.4 %all-to-all-start = ((bf16[16,32,128]{2,1,0:T(8,128)(2,1)}), bf16[16,32,128]{2,1,0:T(8,128)(2,1)S(1)}, u32[]{:S(2)}, u32[]{:S(2)}) async-start(bf16[16,32,128]{2,1,0:T(8,128)(2,1)} %shard_map.119), calls=%async_computation | async-start | bytes 262144 | tf_op jit(solution)/shard_map/all_to_all | solution.py:278
  11.2 0.7 pad_add_fusion.place
  11.8 5.5 %all-to-all-done.got.near = bf16[16,32,128]{2,1,0:T(8,128)(2,1)S(1)} async-done(((bf16[16,32,128]{2,1,0:T(8,128)(2,1)}), bf16[16,32,128]{2,1,0:T(8,128)(2,1)S(1)}, u32[]{:S(2)}, u32[]{:S(2)}) %all-to-all-start) | async-done | bytes 131104 | tf_op jit(solution)/shard_map/all_to_all | solution.py:278
  17.3 0.7 copy-done.1
  18.0 1.8 %shard_map.121 = bf16[8,4,32,128]{3,2,1,0:T(8,128)(2,1)} custom-call(s32[3]{0:T(128)} %pad_add_fusion.place, bf16[16,32,128]{2,1,0:T(8,128)(2,1)} %copy-done.1), custom_call_target="tpu_custom_call" | custom-call | tf_op jit(solution)/shard_map/pallas_call | solution.py:266
  19.7 25.4 %all-to-all-start.1 = ((bf16[8,4,32,128]{3,2,1,0:T(8,128)(2,1)}), bf16[8,4,32,128]{3,2,1,0:T(8,128)(2,1)S(1)}, u32[]{:S(2)}, u32[]{:S(2)}) async-start(bf16[8,4,32,128]{3,2,1,0:T(8,128)(2,1)} %shard_map.121), calls=%async_computation.1 | async-start | bytes 524288 | tf_op jit(solution)/shard_map/all_to_all | solution.py:278
  45.1 0.7 slice.6
  45.8 1.9 %collective-permute-start = (bf16[8,384]{1,0:T(8,128)(2,1)S(1)}, bf16[8,384]{1,0:T(8,128)(2,1)S(1)}, u32[]{:S(2)}, u32[]{:S(2)}) collective-permute-start(bf16[8,384]{1,0:T(8,128)(2,1)S(1)} %slice.6), channel_id=1, source_target_pairs={{0,8},{8,16},{16,24},{24,32},{32,40},{40,48},{48,56},{56,64},{64,7... | collective-permute-start | bytes 18440 | tf_op jit(solution)/shard_map/ppermute | solution.py:284
  47.7 7.0 %shard_map.120 = (bf16[128,384]{1,0:T(8,128)(2,1)}, f32[128,384]{1,0:T(8,128)}, f32[128,384]{1,0:T(8,128)}, f32[128,384]{1,0:T(8,128)}, f32[128,384]{1,0:T(8,128)}, /*index=5*/f32[3,128,128]{2,1,0:T(8,128)}) custom-call(bf16[128,384]{1,0:T(8,128)(2,1)} %queries.3, bf16[128,384]{1,0:T(8,128)(2,1)} %key_rows.3, bf16[128,384]{1,0:T(8,128)(2,1)} %values.3, ...), custom_call_target="tpu_custom_call" | custom-call | tf_op jit(solution)/shard_map/pallas_call | solution.py:266
  54.7 1.4 collective-permute-done.before
  56.1 20.9 %all-to-all-done.1.far = bf16[8,4,32,128]{3,2,1,0:T(8,128)(2,1)S(1)} async-done(((bf16[8,4,32,128]{3,2,1,0:T(8,128)(2,1)}), bf16[8,4,32,128]{3,2,1,0:T(8,128)(2,1)S(1)}, u32[]{:S(2)}, u32[]{:S(2)}) %all-to-all-start.1) | async-done | bytes 262176 | tf_op jit(solution)/shard_map/all_to_all | solution.py:278
  76.9 0.7 copy-done.2
  77.6 1.9 %shard_map.122 = bf16[16,24,128]{2,1,0:T(8,128)(2,1)} custom-call(s32[3]{0:T(128)} %pad_add_fusion.place, bf16[16,32,128]{2,1,0:T(8,128)(2,1)} %copy-done.1, bf16[8,4,32,128]{3,2,1,0:T(8,128)(2,1)} %copy-done.2), custom_call_target="tpu_custom_call" | custom-call | tf_op jit(solution)/shard_map/pallas_call | solution.py:266
  79.5 17.8 %all_to_all.25.ends = bf16[16,24,128]{2,1,0:T(8,128)(2,1)} all-to-all(bf16[16,24,128]{2,1,0:T(8,128)(2,1)} %shard_map.122), channel_id=1, replica_groups=mesh['y'=4,'zh'=8,'zl'=4,'x'=4,'core'=2] {'y','zl'}, dimensions={0} | all-to-all | bytes 196608 | tf_op jit(solution)/shard_map/all_to_all | solution.py:278
  97.3 2.8 %shard_map.123 = (bf16[128,384]{1,0:T(8,128)(2,1)}, bf16[128,384]{1,0:T(8,128)(2,1)}, bf16[128,384]{1,0:T(8,128)(2,1)}, f32[16,4,384]{2,1,0:T(4,128)}) custom-call(bf16[16,24,128]{2,1,0:T(8,128)(2,1)} %all_to_all.25.ends, bf16[128,384]{1,0:T(8,128)(2,1)} %values.3, bf16[128,384]{1,0:T(8,128)(2,1)} %key_rows.3, f32[128,384]{1,0:T(8,128)} %get-tuple-element.39.tail, ...), custom_call_target="tpu_custom_call" | custom-call | tf_op jit(solution)/shard_map/pallas_call | solution.py:266
  100.1 11.3 %all_to_all.26.got = f32[16,4,384]{2,1,0:T(4,128)} all-to-all(f32[16,4,384]{2,1,0:T(4,128)} %get-tuple-element.56), channel_id=1, replica_groups=mesh['y'=4,'zh'=8,'zl'=4,'x'=4,'core'=2] {'y','zl'}, dimensions={0} | all-to-all | bytes 196608 | tf_op jit(solution)/shard_map/all_to_all | solution.py:278
  111.4 1.5 shard_map.126
  112.9 5.9 %all-to-all-start.4 = ((f32[8,4,384]{2,1,0:T(4,128)}), f32[8,4,384]{2,1,0:T(4,128)S(1)}, u32[]{:S(2)}, u32[]{:S(2)}) async-start(f32[8,4,384]{2,1,0:T(4,128)} %shard_map.126), calls=%async_computation.4 | async-start | bytes 98304 | tf_op jit(solution)/shard_map/all_to_all | solution.py:278
  118.8 0.7 slice.7
  119.5 5.7 %collective-permute-start.1 = (bf16[8,384]{1,0:T(8,128)(2,1)S(1)}, bf16[8,384]{1,0:T(8,128)(2,1)S(1)}, u32[]{:S(2)}, u32[]{:S(2)}) collective-permute-start(bf16[8,384]{1,0:T(8,128)(2,1)S(1)} %slice.7), channel_id=1, source_target_pairs={{8,0},{16,8},{24,16},{32,24},{40,32},{48,40},{56,48},{64,56},{72,6... | collective-permute-start | bytes 18440 | tf_op jit(solution)/shard_map/ppermute | solution.py:284
  126.5 1.7 %shard_map.124 = (bf16[16,384]{1,0:T(8,128)(2,1)}, bf16[16,384]{1,0:T(8,128)(2,1)}, bf16[16,384]{1,0:T(8,128)(2,1)}, bf16[16,384]{1,0:T(8,128)(2,1)}, bf16[16,38...) custom-call(s32[3]{0:T(128)} %pad_add_fusion.place, ...), custom_call_target="tpu_custom_call" | custom-call | tf_op jit(solution)/shard_map/pallas_call | solution.py:266
  128.2 6.9 %collective-permute-start.2 = (bf16[16,384]{1,0:T(8,128)(2,1)}, bf16[16,384]{1,0:T(8,128)(2,1)S(1)}, u32[]{:S(2)}, u32[]{:S(2)}) collective-permute-start(bf16[16,384]{1,0:T(8,128)(2,1)} %get-tuple-element.49), channel_id=1, source_target_pairs={{0,1},{1,0},{2,3},{3,2},{4,5},{5,4},{6,7},{7,6},{8,9},{9,8},{10,11... | collective-permute-start | bytes 36872 | tf_op jit(solution)/shard_map/ppermute | solution.py:320
  135.2 3.1 %collective-permute-start.3 = (bf16[16,384]{1,0:T(8,128)(2,1)}, bf16[16,384]{1,0:T(8,128)(2,1)S(1)}, u32[]{:S(2)}, u32[]{:S(2)}) collective-permute-start(bf16[16,384]{1,0:T(8,128)(2,1)} %get-tuple-element.50), channel_id=1, source_target_pairs={{0,2},{1,3},{2,0},{3,1},{4,6},{5,7},{6,4},{7,5},{8,10},{9,11},{10,... | collective-permute-start | bytes 36872 | tf_op jit(solution)/shard_map/ppermute | solution.py:320
  138.3 2.3 %collective-permute-start.4 = (bf16[16,384]{1,0:T(8,128)(2,1)}, bf16[16,384]{1,0:T(8,128)(2,1)S(1)}, u32[]{:S(2)}, u32[]{:S(2)}) collective-permute-start(bf16[16,384]{1,0:T(8,128)(2,1)} %get-tuple-element.51), channel_id=1, source_target_pairs={{0,3},{1,2},{2,1},{3,0},{4,7},{5,6},{6,5},{7,4},{8,11},{9,10},{10,... | collective-permute-start | bytes 36872 | tf_op jit(solution)/shard_map/ppermute | solution.py:320
  140.7 4.7 %collective-permute-start.5 = (bf16[16,384]{1,0:T(8,128)(2,1)}, bf16[16,384]{1,0:T(8,128)(2,1)S(1)}, u32[]{:S(2)}, u32[]{:S(2)}) collective-permute-start(bf16[16,384]{1,0:T(8,128)(2,1)} %get-tuple-element.52), channel_id=1, source_target_pairs={{0,4},{1,5},{2,6},{3,7},{4,0},{5,1},{6,2},{7,3},{8,12},{9,13},{10,... | collective-permute-start | bytes 36872 | tf_op jit(solution)/shard_map/ppermute | solution.py:320
  145.3 2.5 %collective-permute-start.6 = (bf16[16,384]{1,0:T(8,128)(2,1)}, bf16[16,384]{1,0:T(8,128)(2,1)S(1)}, u32[]{:S(2)}, u32[]{:S(2)}) collective-permute-start(bf16[16,384]{1,0:T(8,128)(2,1)} %get-tuple-element.53), channel_id=1, source_target_pairs={{0,5},{1,4},{2,7},{3,6},{4,1},{5,0},{6,3},{7,2},{8,13},{9,12},{10,... | collective-permute-start | bytes 36872 | tf_op jit(solution)/shard_map/ppermute | solution.py:320
  147.9 4.4 %collective-permute-start.7 = (bf16[16,384]{1,0:T(8,128)(2,1)}, bf16[16,384]{1,0:T(8,128)(2,1)S(1)}, u32[]{:S(2)}, u32[]{:S(2)}) collective-permute-start(bf16[16,384]{1,0:T(8,128)(2,1)} %get-tuple-element.54), channel_id=1, source_target_pairs={{0,6},{1,7},{2,4},{3,5},{4,2},{5,3},{6,0},{7,1},{8,14},{9,15},{10,... | collective-permute-start | bytes 36872 | tf_op jit(solution)/shard_map/ppermute | solution.py:320
  152.3 2.3 %collective-permute-start.8 = (bf16[16,384]{1,0:T(8,128)(2,1)S(1)}, bf16[16,384]{1,0:T(8,128)(2,1)S(1)}, u32[]{:S(2)}, u32[]{:S(2)}) collective-permute-start(bf16[16,384]{1,0:T(8,128)(2,1)S(1)} %copy-done.13), channel_id=1, source_target_pairs={{0,7},{1,6},{2,5},{3,4},{4,3},{5,2},{6,1},{7,0},{8,15},{9,14},{10,... | collective-permute-start | bytes 36872 | tf_op jit(solution)/shard_map/ppermute | solution.py:320
  154.7 3.9 %collective-permute-done.8.refs_7_ = bf16[16,384]{1,0:T(8,128)(2,1)S(1)} collective-permute-done((bf16[16,384]{1,0:T(8,128)(2,1)S(1)}, bf16[16,384]{1,0:T(8,128)(2,1)S(1)}, u32[]{:S(2)}, u32[]{:S(2)}) %collective-permute-start.8) | collective-permute-done | bytes 12320 | tf_op jit(solution)/shard_map/ppermute | solution.py:320
  159.1 1.5 shard_map.125
  161.2 1.4 shard_map.127
  (35 shorter events, 2.6 us)
Async XLA Ops:
  0.6 124.6 %copy-start = (f32[4,3072]{1,0:T(4,128)S(1)}, f32[4,3072]{1,0:T(4,128)}, u32[]{:S(2)}) copy-start(f32[4,3072]{1,0:T(4,128)} %param.15) | copy-start | bytes 147460
  2.7 14.6 %all-to-all-start = ((bf16[16,32,128]{2,1,0:T(8,128)(2,1)}), bf16[16,32,128]{2,1,0:T(8,128)(2,1)S(1)}, u32[]{:S(2)}, u32[]{:S(2)}) async-start(bf16[16,32,128]{2,1,0:T(8,128)(2,1)} %shard_map.119), calls=%async_computation | async-start | bytes 262144 | tf_op jit(solution)/shard_map/all_to_all | solution.py:278
  17.3 0.7 copy-start.1
  19.7 57.2 %all-to-all-start.1 = ((bf16[8,4,32,128]{3,2,1,0:T(8,128)(2,1)}), bf16[8,4,32,128]{3,2,1,0:T(8,128)(2,1)S(1)}, u32[]{:S(2)}, u32[]{:S(2)}) async-start(bf16[8,4,32,128]{3,2,1,0:T(8,128)(2,1)} %shard_map.121), calls=%async_computation.1 | async-start | bytes 524288 | tf_op jit(solution)/shard_map/all_to_all | solution.py:278
  45.8 10.3 %collective-permute-start = (bf16[8,384]{1,0:T(8,128)(2,1)S(1)}, bf16[8,384]{1,0:T(8,128)(2,1)S(1)}, u32[]{:S(2)}, u32[]{:S(2)}) collective-permute-start(bf16[8,384]{1,0:T(8,128)(2,1)S(1)} %slice.6), channel_id=1, source_target_pairs={{0,8},{8,16},{16,24},{24,32},{32,40},{40,48},{48,56},{56,64},{64,7... | collective-permute-start | bytes 18440 | tf_op jit(solution)/shard_map/ppermute | solution.py:284
  56.1 23.5 %copy-start.11 = (bf16[8,384]{1,0:T(8,128)(2,1)}, bf16[8,384]{1,0:T(8,128)(2,1)S(1)}, u32[]{:S(2)}) copy-start(bf16[8,384]{1,0:T(8,128)(2,1)S(1)} %collective-permute-done.before) | copy-start | bytes 18436
  76.9 0.7 copy-start.2
  112.9 47.7 %all-to-all-start.4 = ((f32[8,4,384]{2,1,0:T(4,128)}), f32[8,4,384]{2,1,0:T(4,128)S(1)}, u32[]{:S(2)}, u32[]{:S(2)}) async-start(f32[8,4,384]{2,1,0:T(4,128)} %shard_map.126), calls=%async_computation.4 | async-start | bytes 98304 | tf_op jit(solution)/shard_map/all_to_all | solution.py:278
  119.5 6.5 %collective-permute-start.1 = (bf16[8,384]{1,0:T(8,128)(2,1)S(1)}, bf16[8,384]{1,0:T(8,128)(2,1)S(1)}, u32[]{:S(2)}, u32[]{:S(2)}) collective-permute-start(bf16[8,384]{1,0:T(8,128)(2,1)S(1)} %slice.7), channel_id=1, source_target_pairs={{8,0},{16,8},{24,16},{32,24},{40,32},{48,40},{56,48},{64,56},{72,6... | collective-permute-start | bytes 18440 | tf_op jit(solution)/shard_map/ppermute | solution.py:284
  125.9 0.6 copy-start.12
  128.2 24.1 %copy-start.13 = (bf16[16,384]{1,0:T(8,128)(2,1)S(1)}, bf16[16,384]{1,0:T(8,128)(2,1)}, u32[]{:S(2)}) copy-start(bf16[16,384]{1,0:T(8,128)(2,1)} %get-tuple-element.55) | copy-start | bytes 36868
  128.2 19.6 %collective-permute-start.2 = (bf16[16,384]{1,0:T(8,128)(2,1)}, bf16[16,384]{1,0:T(8,128)(2,1)S(1)}, u32[]{:S(2)}, u32[]{:S(2)}) collective-permute-start(bf16[16,384]{1,0:T(8,128)(2,1)} %get-tuple-element.49), channel_id=1, source_target_pairs={{0,1},{1,0},{2,3},{3,2},{4,5},{5,4},{6,7},{7,6},{8,9},{9,8},{10,11... | collective-permute-start | bytes 36872 | tf_op jit(solution)/shard_map/ppermute | solution.py:320
  135.2 17.1 %collective-permute-start.3 = (bf16[16,384]{1,0:T(8,128)(2,1)}, bf16[16,384]{1,0:T(8,128)(2,1)S(1)}, u32[]{:S(2)}, u32[]{:S(2)}) collective-permute-start(bf16[16,384]{1,0:T(8,128)(2,1)} %get-tuple-element.50), channel_id=1, source_target_pairs={{0,2},{1,3},{2,0},{3,1},{4,6},{5,7},{6,4},{7,5},{8,10},{9,11},{10,... | collective-permute-start | bytes 36872 | tf_op jit(solution)/shard_map/ppermute | solution.py:320
  138.3 16.3 %collective-permute-start.4 = (bf16[16,384]{1,0:T(8,128)(2,1)}, bf16[16,384]{1,0:T(8,128)(2,1)S(1)}, u32[]{:S(2)}, u32[]{:S(2)}) collective-permute-start(bf16[16,384]{1,0:T(8,128)(2,1)} %get-tuple-element.51), channel_id=1, source_target_pairs={{0,3},{1,2},{2,1},{3,0},{4,7},{5,6},{6,5},{7,4},{8,11},{9,10},{10,... | collective-permute-start | bytes 36872 | tf_op jit(solution)/shard_map/ppermute | solution.py:320
  140.7 13.9 %collective-permute-start.5 = (bf16[16,384]{1,0:T(8,128)(2,1)}, bf16[16,384]{1,0:T(8,128)(2,1)S(1)}, u32[]{:S(2)}, u32[]{:S(2)}) collective-permute-start(bf16[16,384]{1,0:T(8,128)(2,1)} %get-tuple-element.52), channel_id=1, source_target_pairs={{0,4},{1,5},{2,6},{3,7},{4,0},{5,1},{6,2},{7,3},{8,12},{9,13},{10,... | collective-permute-start | bytes 36872 | tf_op jit(solution)/shard_map/ppermute | solution.py:320
  145.3 9.3 %collective-permute-start.6 = (bf16[16,384]{1,0:T(8,128)(2,1)}, bf16[16,384]{1,0:T(8,128)(2,1)S(1)}, u32[]{:S(2)}, u32[]{:S(2)}) collective-permute-start(bf16[16,384]{1,0:T(8,128)(2,1)} %get-tuple-element.53), channel_id=1, source_target_pairs={{0,5},{1,4},{2,7},{3,6},{4,1},{5,0},{6,3},{7,2},{8,13},{9,12},{10,... | collective-permute-start | bytes 36872 | tf_op jit(solution)/shard_map/ppermute | solution.py:320
  147.9 10.7 %copy-start.4 = (bf16[16,384]{1,0:T(8,128)(2,1)}, bf16[16,384]{1,0:T(8,128)(2,1)S(1)}, u32[]{:S(2)}) copy-start(bf16[16,384]{1,0:T(8,128)(2,1)S(1)} %collective-permute-done.2.refs_1_) | copy-start | bytes 36868
  147.9 6.8 %collective-permute-start.7 = (bf16[16,384]{1,0:T(8,128)(2,1)}, bf16[16,384]{1,0:T(8,128)(2,1)S(1)}, u32[]{:S(2)}, u32[]{:S(2)}) collective-permute-start(bf16[16,384]{1,0:T(8,128)(2,1)} %get-tuple-element.54), channel_id=1, source_target_pairs={{0,6},{1,7},{2,4},{3,5},{4,2},{5,3},{6,0},{7,1},{8,14},{9,15},{10,... | collective-permute-start | bytes 36872 | tf_op jit(solution)/shard_map/ppermute | solution.py:320
  152.3 6.3 %copy-start.5 = (bf16[16,384]{1,0:T(8,128)(2,1)}, bf16[16,384]{1,0:T(8,128)(2,1)S(1)}, u32[]{:S(2)}) copy-start(bf16[16,384]{1,0:T(8,128)(2,1)S(1)} %collective-permute-done.3.refs_2_) | copy-start | bytes 36868
  152.3 6.2 %collective-permute-start.8 = (bf16[16,384]{1,0:T(8,128)(2,1)S(1)}, bf16[16,384]{1,0:T(8,128)(2,1)S(1)}, u32[]{:S(2)}, u32[]{:S(2)}) collective-permute-start(bf16[16,384]{1,0:T(8,128)(2,1)S(1)} %copy-done.13), channel_id=1, source_target_pairs={{0,7},{1,6},{2,5},{3,4},{4,3},{5,2},{6,1},{7,0},{8,15},{9,14},{10,... | collective-permute-start | bytes 36872 | tf_op jit(solution)/shard_map/ppermute | solution.py:320
  154.6 3.9 %copy-start.6 = (bf16[16,384]{1,0:T(8,128)(2,1)}, bf16[16,384]{1,0:T(8,128)(2,1)S(1)}, u32[]{:S(2)}) copy-start(bf16[16,384]{1,0:T(8,128)(2,1)S(1)} %collective-permute-done.4.refs_3_) | copy-start | bytes 36868
  154.6 3.9 %copy-start.7 = (bf16[16,384]{1,0:T(8,128)(2,1)}, bf16[16,384]{1,0:T(8,128)(2,1)S(1)}, u32[]{:S(2)}) copy-start(bf16[16,384]{1,0:T(8,128)(2,1)S(1)} %collective-permute-done.5.refs_4_) | copy-start | bytes 36868
  154.6 3.9 %copy-start.8 = (bf16[16,384]{1,0:T(8,128)(2,1)}, bf16[16,384]{1,0:T(8,128)(2,1)S(1)}, u32[]{:S(2)}) copy-start(bf16[16,384]{1,0:T(8,128)(2,1)S(1)} %collective-permute-done.6.refs_5_) | copy-start | bytes 36868
  154.7 3.9 %copy-start.9 = (bf16[16,384]{1,0:T(8,128)(2,1)}, bf16[16,384]{1,0:T(8,128)(2,1)S(1)}, u32[]{:S(2)}) copy-start(bf16[16,384]{1,0:T(8,128)(2,1)S(1)} %collective-permute-done.7.refs_6_) | copy-start | bytes 36868
  158.5 0.6 copy-start.10
  160.6 0.6 copy-start.3

commit v3 on v2

--- a/solution.py
+++ b/solution.py
@@ -14,6 +14,9 @@
 FAR = 8
 PEERS = 8
 ROWS = 32
+OWN = 8 * HEADS
+FAR_ROWS = 4 * OWN + 8
+APART = 40
 SEQ = ("y", "zh", "zl")
 HEAD = ("x", "core")
 GROUP = ("y", "zl")
@@ -86,42 +89,64 @@
     return [tail[h : h + 1] + tail[HEADS + h : HEADS + h + 1] for h in range(HEADS)]
 
 
-def decays_of(logs, place):
+def decays_of(logs, place, step=0):
+    lane = lax.broadcasted_iota(jnp.int32, (8, WIDTH), 1)
+    row = lax.broadcasted_iota(jnp.int32, (8, WIDTH), 0) + 8 * place
+    decays = []
+    for h in range(HEADS):
+        mine = lane == ((row + step * h) & (WIDTH - 1))
+        picked = jnp.sum(jnp.where(mine, logs[h], 0.0), axis=1, keepdims=True)
+        decays.append(jnp.broadcast_to(jnp.exp(picked), (8, WIDTH)))
+    return jnp.concatenate(decays, axis=0)
+
+
+def run_of(got, place):
+    x = got.astype(F32)
+    logs = logs_of(x[OWN:])
+    return x[:OWN], decays_of(logs, place), logs
+
+
+def packed_of(totals, place):
     lane = lax.broadcasted_iota(jnp.int32, (8, WIDTH), 1)
     row = lax.broadcasted_iota(jnp.int32, (8, WIDTH), 0)
-    mine = lane == row + 8 * place
-    picked = [jnp.sum(jnp.where(mine, logs[h], 0.0), axis=1, keepdims=True) for h in range(HEADS)]
-    return jnp.concatenate([jnp.broadcast_to(jnp.exp(p), (8, WIDTH)) for p in picked], axis=0)
-
-
-def run_of(got, place):
-    x = got.astype(F32)
-    logs = logs_of(x[8 * HEADS :])
-    return x[: 8 * HEADS], decays_of(logs, place), logs
+    packed = jnp.zeros((8, WIDTH), F32)
+    for h in range(HEADS):
+        rows = jnp.zeros((8, WIDTH), F32)
+        for y in range(4):
+            high = totals[y][h].astype(BF16).astype(F32)
+            rows = jnp.where(row == 2 * y, high, rows)
+            rows = jnp.where(row == 2 * y + 1, totals[y][h] - high, rows)
+        rows = jnp.where((lane >> 3) == place, rows, 0.0)
+        packed = packed + (pltpu.roll(rows, APART * h, 1) if h else rows)
+    return packed
 
 
 def group_of(got, place):
-    runs = []
+    runs, totals = [], []
     for y in range(4):
-        running = jnp.zeros((8 * HEADS, WIDTH), F32)
+        running = jnp.zeros((OWN, WIDTH), F32)
         total = [jnp.zeros((1, WIDTH), F32)] * HEADS
         for zl in (3, 2, 1, 0):
             push, decay, logs = run_of(got[y * 4 + zl], place)
             running = push + decay * running
             total = [a + b for a, b in zip(total, logs)]
-        runs.append(jnp.concatenate([running, tail_rows(total)], axis=0).astype(BF16))
-    return runs
+        runs.append(running)
+        totals.append(total)
+    return jnp.concatenate(runs + [packed_of(totals, place)], axis=0).astype(BF16)
 
 
 def ends_of(near, far, place, mine):
     ends = [None] * NEAR
-    running = jnp.zeros((8 * HEADS, WIDTH), F32)
+    every = [far[zh].astype(F32) for zh in range(FAR)]
+    running = jnp.zeros((OWN, WIDTH), F32)
     for y in (3, 2, 1, 0):
-        entering = jnp.zeros((8 * HEADS, WIDTH), F32)
+        entering = jnp.zeros((OWN, WIDTH), F32)
         for zh in range(FAR - 1, -1, -1):
             entering = jnp.where(mine == zh, running, entering)
-            push, decay, _ = run_of(far[zh, y], place)
-            running = push + decay * running
+            at = 4 * OWN + 2 * y
+            logs = every[zh][at : at + 1] + every[zh][at + 1 : at + 2]
+            decay = decays_of([logs] * HEADS, place, APART)
+            running = every[zh][y * OWN : (y + 1) * OWN] + decay * running
         for zl in (3, 2, 1, 0):
             ends[y * 4 + zl] = entering.astype(BF16)
             push, decay, _ = run_of(near[y * 4 + zl], place)
@@ -187,9 +212,8 @@
 
 def group_kernel(place, got, out):
     runs = group_of(got, place[0])
-    for y in range(4):
-        for zh in range(FAR):
-            out[zh, y] = runs[y]
+    for zh in range(FAR):
+        out[zh] = runs
 
 
 def ends_kernel(place, near, far, out):
@@ -290,7 +314,7 @@
     place = jnp.stack([lax.axis_index(GROUP), lax.axis_index("zh"), lax.axis_index(HEAD)]).astype(jnp.int32)
     (sent,) = call(push_kernel, [((NEAR, ROWS, WIDTH), BF16)])(queries, log_gates, grad_output)
     near = exchange(sent, GROUP)
-    (sent,) = call(group_kernel, [((FAR, 4, ROWS, WIDTH), BF16)], 1)(place, near)
+    (sent,) = call(group_kernel, [((FAR, FAR_ROWS, WIDTH), BF16)], 1)(place, near)
     far = exchange(sent, "zh")
     locals_ = call(
         local_kernel, [(wide, BF16), (wide, F32), (wide, F32), (wide, F32), (wide, F32), ((HEADS, WIDTH, WIDTH), F32)]
@@ -298,7 +322,7 @@
     before = passed_along(conv_input[-8:], 1)
     near, before, locals_ = lax.optimization_barrier((near, before, locals_))
     grad_queries, grad_k, grad_v, gate, tail, last = locals_
-    (sent,) = call(ends_kernel, [((NEAR, 8 * HEADS, WIDTH), BF16)], 1)(place, near, far)
+    (sent,) = call(ends_kernel, [((NEAR, OWN, WIDTH), BF16)], 1)(place, near, far)
     ends = exchange(sent, GROUP)
     weights = lax.dynamic_slice_in_dim(conv_kernel, lax.axis_index(HEAD) * columns, columns, 1)
     grad_keys, grad_gates, grad_rows, taps = call(
@@ -316,9 +340,9 @@
         1,
         [pltpu.VMEM((LEN + 8, columns), F32), pltpu.VMEM((PEERS,) + piece, F32)],
     )(place, grad_rows, after, weights)
-    pieces = list(pieces[:1]) + [
-        lax.ppermute(pieces[r], HEAD, [(i, i ^ r) for i in range(PEERS)]) for r in range(1, PEERS)
-    ]
+    sent, pieces = pieces, [pieces[0]]
+    for r in range(1, PEERS):
+        pieces.append(lax.ppermute(sent[r], HEAD, [(i, i ^ r) for i in range(PEERS)]))
     (grad_input,) = call(join_kernel, [((LEN // PEERS, PEERS * columns), BF16)], 1)(place, *pieces)
     (grad_kernel,) = call(total_kernel, [((TAPS, columns), F32)])(summed)
     return (grad_queries, grad_keys, grad_gates, grad_input, grad_kernel)

time: 164 us -> 160 us (0.976)
  blocking collectives: 29 us -> 25.3 us
    all_to_all x2, blocking collectives: 29 us -> 25.3 us  [exchange(): return lax.all_to_all(x, axis, 0, 0, tiled=True)]
  transfers between devices with their start and end apart: 12 -> 12, of which waited for: 5 -> 4; matrix products, arithmetic and copies ran while one was open for 2% -> 2% of each run, Pallas kernels for 6% -> 6%
where the time goes in v3:
time: 160 us; the launch traced here: 159 us
  starting transfers between devices  73.5 us (46%)
  waiting for transfers between devices  31.5 us (20%)
  blocking collectives  25.3 us (16%)
  Pallas kernels  21.6 us (14%)
  local copies, waits for them, and re-layouts  5.14 us (3%)
    all_to_all x3, starting transfers between devices, exchange(): return lax.all_to_all(x, axis, 0, 0, tiled=True)  39.8 us
    all_to_all x3, waiting for transfers between devices, exchange(): return lax.all_to_all(x, axis, 0, 0, tiled=True)  27.5 us
    ppermute x7, starting transfers between devices, per_device(): lax.ppermute(sent[r], HEAD, [(i, i ^ r) for i in range(PEERS)])  26 us
    all_to_all x2, blocking collectives, exchange(): return lax.all_to_all(x, axis, 0, 0, tiled=True)  25.3 us
    pallas_call x9, Pallas kernels, run(): pl.pallas_call(kernel, out_shape=shapes, in_specs=[pl.BlockSpec(memory_sp...  21.6 us
    ppermute x2, starting transfers between devices, passed_along(): return lax.ppermute(x, SEQ, pairs)  7.61 us
    ppermute x7, waiting for transfers between devices, per_device(): lax.ppermute(sent[r], HEAD, [(i, i ^ r) for i in range(PEERS)])  3.87 us
  transfers between devices with their start and end apart: 12, of which 4 were waited for; matrix products, arithmetic and copies ran while one was open for 2% of the time, Pallas kernels for 6%

profile of v3, /device:TPU:9, one launch (start us, length us, event | category | flops | bytes accessed | tf_op | source)
XLA Modules:
  0.0 158.6 jit_solution(602692602189069292)
XLA Ops:
  0.6 2.1 %shard_map.119 = bf16[16,32,128]{2,1,0:T(8,128)(2,1)} custom-call(bf16[128,384]{1,0:T(8,128)(2,1)} %queries.3, bf16[128,384]{1,0:T(8,128)(2,1)} %log_gates.3, bf16[128,384]{1,0:T(8,128)(2,1)} %grad_output.3), custom_call_target="tpu_custom_call" | custom-call | tf_op jit(solution)/shard_map/pallas_call | solution.py:290
  2.7 8.4 %all-to-all-start = ((bf16[16,32,128]{2,1,0:T(8,128)(2,1)}), bf16[16,32,128]{2,1,0:T(8,128)(2,1)S(1)}, u32[]{:S(2)}, u32[]{:S(2)}) async-start(bf16[16,32,128]{2,1,0:T(8,128)(2,1)} %shard_map.119), calls=%async_computation | async-start | bytes 262144 | tf_op jit(solution)/shard_map/all_to_all | solution.py:302
  11.2 0.7 pad_add_fusion.place
  11.8 5.5 %all-to-all-done.got.near = bf16[16,32,128]{2,1,0:T(8,128)(2,1)S(1)} async-done(((bf16[16,32,128]{2,1,0:T(8,128)(2,1)}), bf16[16,32,128]{2,1,0:T(8,128)(2,1)S(1)}, u32[]{:S(2)}, u32[]{:S(2)}) %all-to-all-start) | async-done | bytes 131104 | tf_op jit(solution)/shard_map/all_to_all | solution.py:302
  17.3 0.7 copy-done.1
  18.0 1.7 %shard_map.121 = bf16[8,104,128]{2,1,0:T(8,128)(2,1)} custom-call(s32[3]{0:T(128)} %pad_add_fusion.place, bf16[16,32,128]{2,1,0:T(8,128)(2,1)} %copy-done.1), custom_call_target="tpu_custom_call" | custom-call | tf_op jit(solution)/shard_map/pallas_call | solution.py:290
  19.7 25.4 %all-to-all-start.1 = ((bf16[8,104,128]{2,1,0:T(8,128)(2,1)}), bf16[8,104,128]{2,1,0:T(8,128)(2,1)S(1)}, u32[]{:S(2)}, u32[]{:S(2)}) async-start(bf16[8,104,128]{2,1,0:T(8,128)(2,1)} %shard_map.121), calls=%async_computation.1 | async-start | bytes 425984 | tf_op jit(solution)/shard_map/all_to_all | solution.py:302
  45.1 0.7 slice.6
  45.8 1.9 %collective-permute-start = (bf16[8,384]{1,0:T(8,128)(2,1)S(1)}, bf16[8,384]{1,0:T(8,128)(2,1)S(1)}, u32[]{:S(2)}, u32[]{:S(2)}) collective-permute-start(bf16[8,384]{1,0:T(8,128)(2,1)S(1)} %slice.6), channel_id=1, source_target_pairs={{0,8},{8,16},{16,24},{24,32},{32,40},{40,48},{48,56},{56,64},{64,7... | collective-permute-start | bytes 18440 | tf_op jit(solution)/shard_map/ppermute | solution.py:308
  47.7 7.0 %shard_map.120 = (bf16[128,384]{1,0:T(8,128)(2,1)}, f32[128,384]{1,0:T(8,128)}, f32[128,384]{1,0:T(8,128)}, f32[128,384]{1,0:T(8,128)}, f32[128,384]{1,0:T(8,128)}, /*index=5*/f32[3,128,128]{2,1,0:T(8,128)}) custom-call(bf16[128,384]{1,0:T(8,128)(2,1)} %queries.3, bf16[128,384]{1,0:T(8,128)(2,1)} %key_rows.3, bf16[128,384]{1,0:T(8,128)(2,1)} %values.3, ...), custom_call_target="tpu_custom_call" | custom-call | tf_op jit(solution)/shard_map/pallas_call | solution.py:290
  54.7 22.0 %all-to-all-done.1.far = bf16[8,104,128]{2,1,0:T(8,128)(2,1)S(1)} async-done(((bf16[8,104,128]{2,1,0:T(8,128)(2,1)}), bf16[8,104,128]{2,1,0:T(8,128)(2,1)S(1)}, u32[]{:S(2)}, u32[]{:S(2)}) %all-to-all-start.1) | async-done | bytes 213024 | tf_op jit(solution)/shard_map/all_to_all | solution.py:302
  76.6 0.7 copy-done.2
  77.3 1.9 %shard_map.122 = bf16[16,24,128]{2,1,0:T(8,128)(2,1)} custom-call(s32[3]{0:T(128)} %pad_add_fusion.place, bf16[16,32,128]{2,1,0:T(8,128)(2,1)} %copy-done.1, bf16[8,104,128]{2,1,0:T(8,128)(2,1)} %copy-done.2), custom_call_target="tpu_custom_call" | custom-call | tf_op jit(solution)/shard_map/pallas_call | solution.py:290
  79.2 14.1 %all_to_all.25.ends = bf16[16,24,128]{2,1,0:T(8,128)(2,1)} all-to-all(bf16[16,24,128]{2,1,0:T(8,128)(2,1)} %shard_map.122), channel_id=1, replica_groups=mesh['y'=4,'zh'=8,'zl'=4,'x'=4,'core'=2] {'y','zl'}, dimensions={0} | all-to-all | bytes 196608 | tf_op jit(solution)/shard_map/all_to_all | solution.py:302
  93.3 2.8 %shard_map.123 = (bf16[128,384]{1,0:T(8,128)(2,1)}, bf16[128,384]{1,0:T(8,128)(2,1)}, bf16[128,384]{1,0:T(8,128)(2,1)}, f32[16,4,384]{2,1,0:T(4,128)}) custom-call(bf16[16,24,128]{2,1,0:T(8,128)(2,1)} %all_to_all.25.ends, bf16[128,384]{1,0:T(8,128)(2,1)} %values.3, bf16[128,384]{1,0:T(8,128)(2,1)} %key_rows.3, f32[128,384]{1,0:T(8,128)} %get-tuple-element.39.tail, ...), custom_call_target="tpu_custom_call" | custom-call | tf_op jit(solution)/shard_map/pallas_call | solution.py:290
  96.1 11.3 %all_to_all.26.got = f32[16,4,384]{2,1,0:T(4,128)} all-to-all(f32[16,4,384]{2,1,0:T(4,128)} %get-tuple-element.56), channel_id=1, replica_groups=mesh['y'=4,'zh'=8,'zl'=4,'x'=4,'core'=2] {'y','zl'}, dimensions={0} | all-to-all | bytes 196608 | tf_op jit(solution)/shard_map/all_to_all | solution.py:302
  107.4 1.5 shard_map.126
  108.9 6.0 %all-to-all-start.4 = ((f32[8,4,384]{2,1,0:T(4,128)}), f32[8,4,384]{2,1,0:T(4,128)S(1)}, u32[]{:S(2)}, u32[]{:S(2)}) async-start(f32[8,4,384]{2,1,0:T(4,128)} %shard_map.126), calls=%async_computation.4 | async-start | bytes 98304 | tf_op jit(solution)/shard_map/all_to_all | solution.py:302
  114.9 0.7 slice.7
  115.6 5.7 %collective-permute-start.1 = (bf16[8,384]{1,0:T(8,128)(2,1)S(1)}, bf16[8,384]{1,0:T(8,128)(2,1)S(1)}, u32[]{:S(2)}, u32[]{:S(2)}) collective-permute-start(bf16[8,384]{1,0:T(8,128)(2,1)S(1)} %slice.7), channel_id=1, source_target_pairs={{8,0},{16,8},{24,16},{32,24},{40,32},{48,40},{56,48},{64,56},{72,6... | collective-permute-start | bytes 18440 | tf_op jit(solution)/shard_map/ppermute | solution.py:308
  122.7 1.7 %shard_map.124 = (bf16[16,384]{1,0:T(8,128)(2,1)}, bf16[16,384]{1,0:T(8,128)(2,1)}, bf16[16,384]{1,0:T(8,128)(2,1)}, bf16[16,384]{1,0:T(8,128)(2,1)}, bf16[16,38...) custom-call(s32[3]{0:T(128)} %pad_add_fusion.place, ...), custom_call_target="tpu_custom_call" | custom-call | tf_op jit(solution)/shard_map/pallas_call | solution.py:290
  124.4 6.7 %collective-permute-start.2 = (bf16[16,384]{1,0:T(8,128)(2,1)}, bf16[16,384]{1,0:T(8,128)(2,1)S(1)}, u32[]{:S(2)}, u32[]{:S(2)}) collective-permute-start(bf16[16,384]{1,0:T(8,128)(2,1)} %get-tuple-element.49), channel_id=1, source_target_pairs={{0,1},{1,0},{2,3},{3,2},{4,5},{5,4},{6,7},{7,6},{8,9},{9,8},{10,11... | collective-permute-start | bytes 36872 | tf_op jit(solution)/shard_map/ppermute | solution.py:345
  131.1 3.1 %collective-permute-start.3 = (bf16[16,384]{1,0:T(8,128)(2,1)}, bf16[16,384]{1,0:T(8,128)(2,1)S(1)}, u32[]{:S(2)}, u32[]{:S(2)}) collective-permute-start(bf16[16,384]{1,0:T(8,128)(2,1)} %get-tuple-element.50), channel_id=1, source_target_pairs={{0,2},{1,3},{2,0},{3,1},{4,6},{5,7},{6,4},{7,5},{8,10},{9,11},{10,... | collective-permute-start | bytes 36872 | tf_op jit(solution)/shard_map/ppermute | solution.py:345
  134.3 2.3 %collective-permute-start.4 = (bf16[16,384]{1,0:T(8,128)(2,1)}, bf16[16,384]{1,0:T(8,128)(2,1)S(1)}, u32[]{:S(2)}, u32[]{:S(2)}) collective-permute-start(bf16[16,384]{1,0:T(8,128)(2,1)} %get-tuple-element.51), channel_id=1, source_target_pairs={{0,3},{1,2},{2,1},{3,0},{4,7},{5,6},{6,5},{7,4},{8,11},{9,10},{10,... | collective-permute-start | bytes 36872 | tf_op jit(solution)/shard_map/ppermute | solution.py:345
  136.6 4.7 %collective-permute-start.5 = (bf16[16,384]{1,0:T(8,128)(2,1)}, bf16[16,384]{1,0:T(8,128)(2,1)S(1)}, u32[]{:S(2)}, u32[]{:S(2)}) collective-permute-start(bf16[16,384]{1,0:T(8,128)(2,1)} %get-tuple-element.52), channel_id=1, source_target_pairs={{0,4},{1,5},{2,6},{3,7},{4,0},{5,1},{6,2},{7,3},{8,12},{9,13},{10,... | collective-permute-start | bytes 36872 | tf_op jit(solution)/shard_map/ppermute | solution.py:345
  141.3 2.5 %collective-permute-start.6 = (bf16[16,384]{1,0:T(8,128)(2,1)}, bf16[16,384]{1,0:T(8,128)(2,1)S(1)}, u32[]{:S(2)}, u32[]{:S(2)}) collective-permute-start(bf16[16,384]{1,0:T(8,128)(2,1)} %get-tuple-element.53), channel_id=1, source_target_pairs={{0,5},{1,4},{2,7},{3,6},{4,1},{5,0},{6,3},{7,2},{8,13},{9,12},{10,... | collective-permute-start | bytes 36872 | tf_op jit(solution)/shard_map/ppermute | solution.py:345
  143.8 4.4 %collective-permute-start.7 = (bf16[16,384]{1,0:T(8,128)(2,1)}, bf16[16,384]{1,0:T(8,128)(2,1)S(1)}, u32[]{:S(2)}, u32[]{:S(2)}) collective-permute-start(bf16[16,384]{1,0:T(8,128)(2,1)} %get-tuple-element.54), channel_id=1, source_target_pairs={{0,6},{1,7},{2,4},{3,5},{4,2},{5,3},{6,0},{7,1},{8,14},{9,15},{10,... | collective-permute-start | bytes 36872 | tf_op jit(solution)/shard_map/ppermute | solution.py:345
  148.2 2.3 %collective-permute-start.8 = (bf16[16,384]{1,0:T(8,128)(2,1)S(1)}, bf16[16,384]{1,0:T(8,128)(2,1)S(1)}, u32[]{:S(2)}, u32[]{:S(2)}) collective-permute-start(bf16[16,384]{1,0:T(8,128)(2,1)S(1)} %copy-done.13), channel_id=1, source_target_pairs={{0,7},{1,6},{2,5},{3,4},{4,3},{5,2},{6,1},{7,0},{8,15},{9,14},{10,... | collective-permute-start | bytes 36872 | tf_op jit(solution)/shard_map/ppermute | solution.py:345
  150.6 3.9 %collective-permute-done.8.refs_7_ = bf16[16,384]{1,0:T(8,128)(2,1)S(1)} collective-permute-done((bf16[16,384]{1,0:T(8,128)(2,1)S(1)}, bf16[16,384]{1,0:T(8,128)(2,1)S(1)}, u32[]{:S(2)}, u32[]{:S(2)}) %collective-permute-start.8) | collective-permute-done | bytes 12320 | tf_op jit(solution)/shard_map/ppermute | solution.py:345
  155.1 1.5 shard_map.125
  156.6 0.6 copy-done.3
  157.2 1.4 shard_map.127
  (35 shorter events, 2.0 us)
Async XLA Ops:
  0.6 120.7 %copy-start = (f32[4,3072]{1,0:T(4,128)S(1)}, f32[4,3072]{1,0:T(4,128)}, u32[]{:S(2)}) copy-start(f32[4,3072]{1,0:T(4,128)} %param.15) | copy-start | bytes 147460
  2.7 14.6 %all-to-all-start = ((bf16[16,32,128]{2,1,0:T(8,128)(2,1)}), bf16[16,32,128]{2,1,0:T(8,128)(2,1)S(1)}, u32[]{:S(2)}, u32[]{:S(2)}) async-start(bf16[16,32,128]{2,1,0:T(8,128)(2,1)} %shard_map.119), calls=%async_computation | async-start | bytes 262144 | tf_op jit(solution)/shard_map/all_to_all | solution.py:302
  17.3 0.7 copy-start.1
  19.7 56.9 %all-to-all-start.1 = ((bf16[8,104,128]{2,1,0:T(8,128)(2,1)}), bf16[8,104,128]{2,1,0:T(8,128)(2,1)S(1)}, u32[]{:S(2)}, u32[]{:S(2)}) async-start(bf16[8,104,128]{2,1,0:T(8,128)(2,1)} %shard_map.121), calls=%async_computation.1 | async-start | bytes 425984 | tf_op jit(solution)/shard_map/all_to_all | solution.py:302
  45.8 8.9 %collective-permute-start = (bf16[8,384]{1,0:T(8,128)(2,1)S(1)}, bf16[8,384]{1,0:T(8,128)(2,1)S(1)}, u32[]{:S(2)}, u32[]{:S(2)}) collective-permute-start(bf16[8,384]{1,0:T(8,128)(2,1)S(1)} %slice.6), channel_id=1, source_target_pairs={{0,8},{8,16},{16,24},{24,32},{32,40},{40,48},{48,56},{56,64},{64,7... | collective-permute-start | bytes 18440 | tf_op jit(solution)/shard_map/ppermute | solution.py:308
  54.7 24.5 %copy-start.11 = (bf16[8,384]{1,0:T(8,128)(2,1)}, bf16[8,384]{1,0:T(8,128)(2,1)S(1)}, u32[]{:S(2)}) copy-start(bf16[8,384]{1,0:T(8,128)(2,1)S(1)} %collective-permute-done.before) | copy-start | bytes 18436
  76.6 0.7 copy-start.2
  108.9 47.7 %all-to-all-start.4 = ((f32[8,4,384]{2,1,0:T(4,128)}), f32[8,4,384]{2,1,0:T(4,128)S(1)}, u32[]{:S(2)}, u32[]{:S(2)}) async-start(f32[8,4,384]{2,1,0:T(4,128)} %shard_map.126), calls=%async_computation.4 | async-start | bytes 98304 | tf_op jit(solution)/shard_map/all_to_all | solution.py:302
  115.6 6.5 %collective-permute-start.1 = (bf16[8,384]{1,0:T(8,128)(2,1)S(1)}, bf16[8,384]{1,0:T(8,128)(2,1)S(1)}, u32[]{:S(2)}, u32[]{:S(2)}) collective-permute-start(bf16[8,384]{1,0:T(8,128)(2,1)S(1)} %slice.7), channel_id=1, source_target_pairs={{8,0},{16,8},{24,16},{32,24},{40,32},{48,40},{56,48},{64,56},{72,6... | collective-permute-start | bytes 18440 | tf_op jit(solution)/shard_map/ppermute | solution.py:308
  122.1 0.6 copy-start.12
  124.4 23.8 %copy-start.13 = (bf16[16,384]{1,0:T(8,128)(2,1)S(1)}, bf16[16,384]{1,0:T(8,128)(2,1)}, u32[]{:S(2)}) copy-start(bf16[16,384]{1,0:T(8,128)(2,1)} %get-tuple-element.55) | copy-start | bytes 36868
  124.4 19.4 %collective-permute-start.2 = (bf16[16,384]{1,0:T(8,128)(2,1)}, bf16[16,384]{1,0:T(8,128)(2,1)S(1)}, u32[]{:S(2)}, u32[]{:S(2)}) collective-permute-start(bf16[16,384]{1,0:T(8,128)(2,1)} %get-tuple-element.49), channel_id=1, source_target_pairs={{0,1},{1,0},{2,3},{3,2},{4,5},{5,4},{6,7},{7,6},{8,9},{9,8},{10,11... | collective-permute-start | bytes 36872 | tf_op jit(solution)/shard_map/ppermute | solution.py:345
  131.1 17.1 %collective-permute-start.3 = (bf16[16,384]{1,0:T(8,128)(2,1)}, bf16[16,384]{1,0:T(8,128)(2,1)S(1)}, u32[]{:S(2)}, u32[]{:S(2)}) collective-permute-start(bf16[16,384]{1,0:T(8,128)(2,1)} %get-tuple-element.50), channel_id=1, source_target_pairs={{0,2},{1,3},{2,0},{3,1},{4,6},{5,7},{6,4},{7,5},{8,10},{9,11},{10,... | collective-permute-start | bytes 36872 | tf_op jit(solution)/shard_map/ppermute | solution.py:345
  134.3 16.3 %collective-permute-start.4 = (bf16[16,384]{1,0:T(8,128)(2,1)}, bf16[16,384]{1,0:T(8,128)(2,1)S(1)}, u32[]{:S(2)}, u32[]{:S(2)}) collective-permute-start(bf16[16,384]{1,0:T(8,128)(2,1)} %get-tuple-element.51), channel_id=1, source_target_pairs={{0,3},{1,2},{2,1},{3,0},{4,7},{5,6},{6,5},{7,4},{8,11},{9,10},{10,... | collective-permute-start | bytes 36872 | tf_op jit(solution)/shard_map/ppermute | solution.py:345
  136.6 13.9 %collective-permute-start.5 = (bf16[16,384]{1,0:T(8,128)(2,1)}, bf16[16,384]{1,0:T(8,128)(2,1)S(1)}, u32[]{:S(2)}, u32[]{:S(2)}) collective-permute-start(bf16[16,384]{1,0:T(8,128)(2,1)} %get-tuple-element.52), channel_id=1, source_target_pairs={{0,4},{1,5},{2,6},{3,7},{4,0},{5,1},{6,2},{7,3},{8,12},{9,13},{10,... | collective-permute-start | bytes 36872 | tf_op jit(solution)/shard_map/ppermute | solution.py:345
  141.3 9.3 %collective-permute-start.6 = (bf16[16,384]{1,0:T(8,128)(2,1)}, bf16[16,384]{1,0:T(8,128)(2,1)S(1)}, u32[]{:S(2)}, u32[]{:S(2)}) collective-permute-start(bf16[16,384]{1,0:T(8,128)(2,1)} %get-tuple-element.53), channel_id=1, source_target_pairs={{0,5},{1,4},{2,7},{3,6},{4,1},{5,0},{6,3},{7,2},{8,13},{9,12},{10,... | collective-permute-start | bytes 36872 | tf_op jit(solution)/shard_map/ppermute | solution.py:345
  143.8 10.7 %copy-start.4 = (bf16[16,384]{1,0:T(8,128)(2,1)}, bf16[16,384]{1,0:T(8,128)(2,1)S(1)}, u32[]{:S(2)}) copy-start(bf16[16,384]{1,0:T(8,128)(2,1)S(1)} %collective-permute-done.2.refs_1_) | copy-start | bytes 36868
  143.8 6.8 %collective-permute-start.7 = (bf16[16,384]{1,0:T(8,128)(2,1)}, bf16[16,384]{1,0:T(8,128)(2,1)S(1)}, u32[]{:S(2)}, u32[]{:S(2)}) collective-permute-start(bf16[16,384]{1,0:T(8,128)(2,1)} %get-tuple-element.54), channel_id=1, source_target_pairs={{0,6},{1,7},{2,4},{3,5},{4,2},{5,3},{6,0},{7,1},{8,14},{9,15},{10,... | collective-permute-start | bytes 36872 | tf_op jit(solution)/shard_map/ppermute | solution.py:345
  148.2 6.3 %copy-start.5 = (bf16[16,384]{1,0:T(8,128)(2,1)}, bf16[16,384]{1,0:T(8,128)(2,1)S(1)}, u32[]{:S(2)}) copy-start(bf16[16,384]{1,0:T(8,128)(2,1)S(1)} %collective-permute-done.3.refs_2_) | copy-start | bytes 36868
  148.2 6.2 %collective-permute-start.8 = (bf16[16,384]{1,0:T(8,128)(2,1)S(1)}, bf16[16,384]{1,0:T(8,128)(2,1)S(1)}, u32[]{:S(2)}, u32[]{:S(2)}) collective-permute-start(bf16[16,384]{1,0:T(8,128)(2,1)S(1)} %copy-done.13), channel_id=1, source_target_pairs={{0,7},{1,6},{2,5},{3,4},{4,3},{5,2},{6,1},{7,0},{8,15},{9,14},{10,... | collective-permute-start | bytes 36872 | tf_op jit(solution)/shard_map/ppermute | solution.py:345
  150.5 3.9 %copy-start.6 = (bf16[16,384]{1,0:T(8,128)(2,1)}, bf16[16,384]{1,0:T(8,128)(2,1)S(1)}, u32[]{:S(2)}) copy-start(bf16[16,384]{1,0:T(8,128)(2,1)S(1)} %collective-permute-done.4.refs_3_) | copy-start | bytes 36868
  150.6 3.9 %copy-start.7 = (bf16[16,384]{1,0:T(8,128)(2,1)}, bf16[16,384]{1,0:T(8,128)(2,1)S(1)}, u32[]{:S(2)}) copy-start(bf16[16,384]{1,0:T(8,128)(2,1)S(1)} %collective-permute-done.5.refs_4_) | copy-start | bytes 36868
  150.6 3.9 %copy-start.8 = (bf16[16,384]{1,0:T(8,128)(2,1)}, bf16[16,384]{1,0:T(8,128)(2,1)S(1)}, u32[]{:S(2)}) copy-start(bf16[16,384]{1,0:T(8,128)(2,1)S(1)} %collective-permute-done.6.refs_5_) | copy-start | bytes 36868
  150.6 3.9 %copy-start.9 = (bf16[16,384]{1,0:T(8,128)(2,1)}, bf16[16,384]{1,0:T(8,128)(2,1)S(1)}, u32[]{:S(2)}) copy-start(bf16[16,384]{1,0:T(8,128)(2,1)S(1)} %collective-permute-done.7.refs_6_) | copy-start | bytes 36868
  154.5 0.6 copy-start.10
  156.6 0.6 copy-start.3

commit v4 on v3

--- a/solution.py
+++ b/solution.py
@@ -254,32 +254,34 @@
             taps[:, tap : tap + 1, at] = jnp.broadcast_to(term[None], (NEAR, 1, WIDTH))
 
 
-def conv_kernel_body(place, grad_v, after, weights, *outs):
-    outs, padded, rows = outs[:PEERS], outs[PEERS], outs[PEERS + 1]
+def conv_kernel_body(place, grad_v, after, weights, mine, other, padded, rows):
     padded[:LEN] = grad_v[...].astype(F32)
     padded[LEN:] = after[...].astype(F32)
     total = weights[0:1] * padded[0:LEN]
     for tap in range(1, TAPS):
         total = total + weights[tap : tap + 1] * padded[tap : tap + LEN]
     rows[...] = total.reshape(PEERS, LEN // PEERS, HEADS * WIDTH)
-    for r in range(PEERS):
-        outs[r][...] = rows[place[2] ^ r].astype(BF16)
-
-
-def join_kernel(place, *refs):
-    out = refs[PEERS]
-    for r in range(PEERS):
-        start = pl.multiple_of((place[2] ^ r) * (HEADS * WIDTH), WIDTH)
-        out[:, pl.ds(start, HEADS * WIDTH)] = refs[r][...]
-
-
-def spread_kernel(got, out):
-    total = jnp.sum(got[...], axis=0)
-    out[...] = jnp.broadcast_to(total[None], out.shape)
-
-
-def total_kernel(got, out):
-    out[...] = jnp.sum(got[...], axis=0)
+    for r in range(PEERS // 2):
+        mine[r] = rows[place[2] ^ (2 * r)].astype(BF16)
+        other[r] = rows[place[2] ^ (2 * r + 1)].astype(BF16)
+
+
+def pack_kernel(mine, other, *outs):
+    for r in range(1, PEERS // 2):
+        outs[r - 1][0] = mine[r]
+        outs[r - 1][1] = other[r]
+
+
+def join_kernel(place, mine, other, *refs):
+    out = refs[PEERS // 2 - 1]
+    for r in range(PEERS // 2):
+        for core in (0, 1):
+            if r:
+                piece = refs[r - 1][core]
+            else:
+                piece = (mine, other)[core][0]
+            start = pl.multiple_of((place[2] ^ (2 * r + core)) * (HEADS * WIDTH), WIDTH)
+            out[:, pl.ds(start, HEADS * WIDTH)] = piece
 
 
 def call(kernel, outs, scalars=0, scratch=()):
@@ -330,21 +332,24 @@
         [(wide, BF16), (wide, BF16), (wide, BF16), ((NEAR, TAPS, columns), F32)],
         scratch=[pltpu.VMEM((LEN + 8, columns), F32)],
     )(ends, values, key_rows, tail, grad_k, grad_v, gate, last, conv_input, before)
-    (taps,) = call(spread_kernel, [((FAR, TAPS, columns), F32)])(exchange(taps, GROUP))
-    summed = exchange(taps, "zh")
+    taps = jnp.sum(exchange(taps, GROUP), axis=0)
+    summed = exchange(jnp.broadcast_to(taps[None], (FAR, TAPS, columns)), "zh")
     after = passed_along(grad_rows[:8], -1)
     piece = (LEN // PEERS, columns)
-    pieces = call(
+    half = PEERS // 2
+    mine, other = call(
         conv_kernel_body,
-        [(piece, BF16)] * PEERS,
+        [((half,) + piece, BF16)] * 2,
         1,
         [pltpu.VMEM((LEN + 8, columns), F32), pltpu.VMEM((PEERS,) + piece, F32)],
     )(place, grad_rows, after, weights)
-    sent, pieces = pieces, [pieces[0]]
-    for r in range(1, PEERS):
-        pieces.append(lax.ppermute(sent[r], HEAD, [(i, i ^ r) for i in range(PEERS)]))
-    (grad_input,) = call(join_kernel, [((LEN // PEERS, PEERS * columns), BF16)], 1)(place, *pieces)
-    (grad_kernel,) = call(total_kernel, [((TAPS, columns), F32)])(summed)
+    other = lax.ppermute(other, HEAD, [(i, i ^ 1) for i in range(PEERS)])
+    sent = call(pack_kernel, [((2,) + piece, BF16)] * (half - 1))(mine, other)
+    pieces = [
+        lax.ppermute(sent[r - 1], HEAD, [(i, i ^ (2 * r)) for i in range(PEERS)]) for r in range(1, half)
+    ]
+    (grad_input,) = call(join_kernel, [((LEN // PEERS, PEERS * columns), BF16)], 1)(place, mine, other, *pieces)
+    grad_kernel = jnp.sum(summed, axis=0)
     return (grad_queries, grad_keys, grad_gates, grad_input, grad_kernel)
 
 

time: 160 us -> 151 us (0.944)
  the two profiles are of different devices: /device:TPU:9 before, /device:TPU:8 now
where the time goes in v4:
time: 151 us; the launch traced here: 150 us
  starting transfers between devices  59.2 us (39%)
  waiting for transfers between devices  38.4 us (25%)
  blocking collectives  24.6 us (16%)
  Pallas kernels  20.1 us (13%)
  local copies, waits for them, and re-layouts  5.77 us (4%)
    all_to_all x3, starting transfers between devices, exchange(): return lax.all_to_all(x, axis, 0, 0, tiled=True)  38.6 us
    all_to_all x2, blocking collectives, exchange(): return lax.all_to_all(x, axis, 0, 0, tiled=True)  24.6 us
    all_to_all x3, waiting for transfers between devices, exchange(): return lax.all_to_all(x, axis, 0, 0, tiled=True)  23.2 us
    pallas_call x8, Pallas kernels, run(): pl.pallas_call(kernel, out_shape=shapes, in_specs=[pl.BlockSpec(memory_sp...  20.1 us
    ppermute x3, starting transfers between devices, per_device(): lax.ppermute(sent[r - 1], HEAD, [(i, i ^ 2 * r) for i in range(PEERS)])  10.4 us
    ppermute x2, waiting for transfers between devices, passed_along(): return lax.ppermute(x, SEQ, pairs)  9.09 us
    ppermute x2, starting transfers between devices, passed_along(): return lax.ppermute(x, SEQ, pairs)  8.29 us
    ppermute x3, waiting for transfers between devices, per_device(): lax.ppermute(sent[r - 1], HEAD, [(i, i ^ 2 * r) for i in range(PEERS)])  4.73 us
  transfers between devices with their start and end apart: 9, of which 7 were waited for; matrix products, arithmetic and copies ran while one was open for 2% of the time, Pallas kernels for 8%

profile of v4, /device:TPU:8, one launch (start us, length us, event | category | flops | bytes accessed | tf_op | source)
XLA Modules:
  0.0 150.1 jit_solution(6067979286688942613)
XLA Ops:
  0.6 2.1 %shard_map.119 = bf16[16,32,128]{2,1,0:T(8,128)(2,1)} custom-call(bf16[128,384]{1,0:T(8,128)(2,1)} %queries.3, bf16[128,384]{1,0:T(8,128)(2,1)} %log_gates.3, bf16[128,384]{1,0:T(8,128)(2,1)} %grad_output.3), custom_call_target="tpu_custom_call" | custom-call | tf_op jit(solution)/shard_map/pallas_call | solution.py:292
  2.7 16.4 %all-to-all-start = ((bf16[16,32,128]{2,1,0:T(8,128)(2,1)}), bf16[16,32,128]{2,1,0:T(8,128)(2,1)S(1)}, u32[]{:S(2)}, u32[]{:S(2)}) async-start(bf16[16,32,128]{2,1,0:T(8,128)(2,1)} %shard_map.119), calls=%async_computation | async-start | bytes 262144 | tf_op jit(solution)/shard_map/all_to_all | solution.py:304
  19.1 0.7 pad_add_fusion.place
  19.8 6.4 %all-to-all-done.got.near = bf16[16,32,128]{2,1,0:T(8,128)(2,1)S(1)} async-done(((bf16[16,32,128]{2,1,0:T(8,128)(2,1)}), bf16[16,32,128]{2,1,0:T(8,128)(2,1)S(1)}, u32[]{:S(2)}, u32[]{:S(2)}) %all-to-all-start) | async-done | bytes 131104 | tf_op jit(solution)/shard_map/all_to_all | solution.py:304
  26.2 0.6 copy-done.1
  26.9 1.7 %shard_map.121 = bf16[8,104,128]{2,1,0:T(8,128)(2,1)} custom-call(s32[3]{0:T(128)} %pad_add_fusion.place, bf16[16,32,128]{2,1,0:T(8,128)(2,1)} %copy-done.1), custom_call_target="tpu_custom_call" | custom-call | tf_op jit(solution)/shard_map/pallas_call | solution.py:292
  28.6 18.2 %all-to-all-start.1 = ((bf16[8,104,128]{2,1,0:T(8,128)(2,1)}), bf16[8,104,128]{2,1,0:T(8,128)(2,1)S(1)}, u32[]{:S(2)}, u32[]{:S(2)}) async-start(bf16[8,104,128]{2,1,0:T(8,128)(2,1)} %shard_map.121), calls=%async_computation.1 | async-start | bytes 425984 | tf_op jit(solution)/shard_map/all_to_all | solution.py:304
  46.8 0.7 slice.6
  47.5 2.0 %collective-permute-start = (bf16[8,384]{1,0:T(8,128)(2,1)S(1)}, bf16[8,384]{1,0:T(8,128)(2,1)S(1)}, u32[]{:S(2)}, u32[]{:S(2)}) collective-permute-start(bf16[8,384]{1,0:T(8,128)(2,1)S(1)} %slice.6), channel_id=1, source_target_pairs={{0,8},{8,16},{16,24},{24,32},{32,40},{40,48},{48,56},{56,64},{64,7... | collective-permute-start | bytes 18440 | tf_op jit(solution)/shard_map/ppermute | solution.py:310
  49.5 7.0 %shard_map.120 = (bf16[128,384]{1,0:T(8,128)(2,1)}, f32[128,384]{1,0:T(8,128)}, f32[128,384]{1,0:T(8,128)}, f32[128,384]{1,0:T(8,128)}, f32[128,384]{1,0:T(8,128)}, /*index=5*/f32[3,128,128]{2,1,0:T(8,128)}) custom-call(bf16[128,384]{1,0:T(8,128)(2,1)} %queries.3, bf16[128,384]{1,0:T(8,128)(2,1)} %key_rows.3, bf16[128,384]{1,0:T(8,128)(2,1)} %values.3, ...), custom_call_target="tpu_custom_call" | custom-call | tf_op jit(solution)/shard_map/pallas_call | solution.py:292
  56.5 8.4 %collective-permute-done.before = bf16[8,384]{1,0:T(8,128)(2,1)S(1)} collective-permute-done((bf16[8,384]{1,0:T(8,128)(2,1)S(1)}, bf16[8,384]{1,0:T(8,128)(2,1)S(1)}, u32[]{:S(2)}, u32[]{:S(2)}) %collective-permute-start) | collective-permute-done | bytes 6176 | tf_op jit(solution)/shard_map/ppermute | solution.py:310
  64.8 16.7 %all-to-all-done.1.far = bf16[8,104,128]{2,1,0:T(8,128)(2,1)S(1)} async-done(((bf16[8,104,128]{2,1,0:T(8,128)(2,1)}), bf16[8,104,128]{2,1,0:T(8,128)(2,1)S(1)}, u32[]{:S(2)}, u32[]{:S(2)}) %all-to-all-start.1) | async-done | bytes 213024 | tf_op jit(solution)/shard_map/all_to_all | solution.py:304
  81.6 0.7 copy-done.2
  82.2 1.9 %shard_map.122 = bf16[16,24,128]{2,1,0:T(8,128)(2,1)} custom-call(s32[3]{0:T(128)} %pad_add_fusion.place, bf16[16,32,128]{2,1,0:T(8,128)(2,1)} %copy-done.1, bf16[8,104,128]{2,1,0:T(8,128)(2,1)} %copy-done.2), custom_call_target="tpu_custom_call" | custom-call | tf_op jit(solution)/shard_map/pallas_call | solution.py:292
  84.1 12.9 %all_to_all.25.ends = bf16[16,24,128]{2,1,0:T(8,128)(2,1)} all-to-all(bf16[16,24,128]{2,1,0:T(8,128)(2,1)} %shard_map.122), channel_id=1, replica_groups=mesh['y'=4,'zh'=8,'zl'=4,'x'=4,'core'=2] {'y','zl'}, dimensions={0} | all-to-all | bytes 196608 | tf_op jit(solution)/shard_map/all_to_all | solution.py:304
  97.0 2.8 %shard_map.123 = (bf16[128,384]{1,0:T(8,128)(2,1)}, bf16[128,384]{1,0:T(8,128)(2,1)}, bf16[128,384]{1,0:T(8,128)(2,1)}, f32[16,4,384]{2,1,0:T(4,128)}) custom-call(bf16[16,24,128]{2,1,0:T(8,128)(2,1)} %all_to_all.25.ends, bf16[128,384]{1,0:T(8,128)(2,1)} %values.3, bf16[128,384]{1,0:T(8,128)(2,1)} %key_rows.3, f32[128,384]{1,0:T(8,128)} %get-tuple-element.36.tail, ...), custom_call_target="tpu_custom_call" | custom-call | tf_op jit(solution)/shard_map/pallas_call | solution.py:292
  99.8 11.7 %all_to_all.26 = f32[16,4,384]{2,1,0:T(4,128)S(1)} all-to-all(f32[16,4,384]{2,1,0:T(4,128)} %get-tuple-element.50), channel_id=1, replica_groups=mesh['y'=4,'zh'=8,'zl'=4,'x'=4,'core'=2] {'y','zl'}, dimensions={0} | all-to-all | bytes 196608 | tf_op jit(solution)/shard_map/all_to_all | solution.py:304
  111.5 0.6 broadcast_in_dim.2
  112.2 4.1 %all-to-all-start.4 = ((f32[8,4,384]{2,1,0:T(4,128)}), f32[8,4,384]{2,1,0:T(4,128)S(1)}, u32[]{:S(2)}, u32[]{:S(2)}) async-start(f32[8,4,384]{2,1,0:T(4,128)} %broadcast_in_dim.2), calls=%async_computation.4 | async-start | bytes 98304 | tf_op jit(solution)/shard_map/all_to_all | solution.py:304
  116.2 0.7 slice.7
  116.9 6.3 %collective-permute-start.1 = (bf16[8,384]{1,0:T(8,128)(2,1)S(1)}, bf16[8,384]{1,0:T(8,128)(2,1)S(1)}, u32[]{:S(2)}, u32[]{:S(2)}) collective-permute-start(bf16[8,384]{1,0:T(8,128)(2,1)S(1)} %slice.7), channel_id=1, source_target_pairs={{8,0},{16,8},{24,16},{32,24},{40,32},{48,40},{56,48},{64,56},{72,6... | collective-permute-start | bytes 18440 | tf_op jit(solution)/shard_map/ppermute | solution.py:310
  123.8 0.7 collective-permute-done.1.after
  125.1 1.7 %shard_map.124 = (bf16[4,16,384]{2,1,0:T(8,128)(2,1)}, bf16[4,16,384]{2,1,0:T(8,128)(2,1)}) custom-call(s32[3]{0:T(128)} %pad_add_fusion.place, bf16[128,384]{1,0:T(8,128)(2,1)} %get-tuple-element.44.grad_v, bf16[8,384]{1,0:T(8,128)(2,1)} %copy-done.8, f32[4,384]{1,0:T(4,128)} %constant_dynamic-slice_fusion.weights), custom_call_target="tpu_custom_call" | custom-call | tf_op jit(solution)/shard_map/pallas_call | solution.py:292
  126.8 1.9 %collective-permute-start.2 = (bf16[4,16,384]{2,1,0:T(8,128)(2,1)}, bf16[4,16,384]{2,1,0:T(8,128)(2,1)S(1)}, u32[]{:S(2)}, u32[]{:S(2)}) collective-permute-start(bf16[4,16,384]{2,1,0:T(8,128)(2,1)} %get-tuple-element.46), channel_id=1, source_target_pairs={{0,1},{1,0},{2,3},{3,2},{4,5},{5,4},{6,7},{7,6},{8,9},{9,8},{10,11... | collective-permute-start | bytes 147464 | tf_op jit(solution)/shard_map/ppermute | solution.py:346
  128.7 1.4 collective-permute-done.2.other
  130.1 0.6 copy-done.3
  130.8 1.5 shard_map.125
  132.2 3.4 %collective-permute-start.3 = (bf16[2,16,384]{2,1,0:T(8,128)(2,1)}, bf16[2,16,384]{2,1,0:T(8,128)(2,1)S(1)}, u32[]{:S(2)}, u32[]{:S(2)}) collective-permute-start(bf16[2,16,384]{2,1,0:T(8,128)(2,1)} %get-tuple-element.47), channel_id=1, source_target_pairs={{0,2},{1,3},{2,0},{3,1},{4,6},{5,7},{6,4},{7,5},{8,10},{9,11},{10,... | collective-permute-start | bytes 73736 | tf_op jit(solution)/shard_map/ppermute | solution.py:349
  135.6 4.6 %collective-permute-start.4 = (bf16[2,16,384]{2,1,0:T(8,128)(2,1)}, bf16[2,16,384]{2,1,0:T(8,128)(2,1)S(1)}, u32[]{:S(2)}, u32[]{:S(2)}) collective-permute-start(bf16[2,16,384]{2,1,0:T(8,128)(2,1)} %get-tuple-element.48), channel_id=1, source_target_pairs={{0,4},{1,5},{2,6},{3,7},{4,0},{5,1},{6,2},{7,3},{8,12},{9,13},{10,... | collective-permute-start | bytes 73736 | tf_op jit(solution)/shard_map/ppermute | solution.py:349
  140.3 2.4 %collective-permute-start.5 = (bf16[2,16,384]{2,1,0:T(8,128)(2,1)}, bf16[2,16,384]{2,1,0:T(8,128)(2,1)S(1)}, u32[]{:S(2)}, u32[]{:S(2)}) collective-permute-start(bf16[2,16,384]{2,1,0:T(8,128)(2,1)} %get-tuple-element.49), channel_id=1, source_target_pairs={{0,6},{1,7},{2,4},{3,5},{4,2},{5,3},{6,0},{7,1},{8,14},{9,15},{10,... | collective-permute-start | bytes 73736 | tf_op jit(solution)/shard_map/ppermute | solution.py:349
  143.1 4.3 %collective-permute-done.5.refs_2_ = bf16[2,16,384]{2,1,0:T(8,128)(2,1)S(1)} collective-permute-done((bf16[2,16,384]{2,1,0:T(8,128)(2,1)}, bf16[2,16,384]{2,1,0:T(8,128)(2,1)S(1)}, u32[]{:S(2)}, u32[]{:S(2)}) %collective-permute-start.5) | collective-permute-done | bytes 24608 | tf_op jit(solution)/shard_map/ppermute | solution.py:349
  148.0 1.5 %shard_map.126 = bf16[16,3072]{1,0:T(8,128)(2,1)} custom-call(s32[3]{0:T(128)} %pad_add_fusion.place, bf16[4,16,384]{2,1,0:T(8,128)(2,1)} %get-tuple-element.45.mine, bf16[4,16,384]{2,1,0:T(8,128)(2,1)} %copy-done.3, bf16[2,16,384]{2,1,0:T(8,128)(2,1)} %copy-done.4, bf16[2,16,384]{2,1,0:T(8,128)(2,1)} %copy-done.5, bf16[2,16,384]{2,1,0:T(8,128)(2,1)} %copy-done.6), custom_call_target="tpu_custom_call" | custom-call | tf_op jit(solution)/shard_map/pallas_call | solution.py:292
  (21 shorter events, 2.9 us)
Async XLA Ops:
  0.6 122.6 %copy-start = (f32[4,3072]{1,0:T(4,128)S(1)}, f32[4,3072]{1,0:T(4,128)}, u32[]{:S(2)}) copy-start(f32[4,3072]{1,0:T(4,128)} %param.15) | copy-start | bytes 147460
  2.7 23.5 %all-to-all-start = ((bf16[16,32,128]{2,1,0:T(8,128)(2,1)}), bf16[16,32,128]{2,1,0:T(8,128)(2,1)S(1)}, u32[]{:S(2)}, u32[]{:S(2)}) async-start(bf16[16,32,128]{2,1,0:T(8,128)(2,1)} %shard_map.119), calls=%async_computation | async-start | bytes 262144 | tf_op jit(solution)/shard_map/all_to_all | solution.py:304
  26.2 0.6 copy-start.1
  28.6 53.0 %all-to-all-start.1 = ((bf16[8,104,128]{2,1,0:T(8,128)(2,1)}), bf16[8,104,128]{2,1,0:T(8,128)(2,1)S(1)}, u32[]{:S(2)}, u32[]{:S(2)}) async-start(bf16[8,104,128]{2,1,0:T(8,128)(2,1)} %shard_map.121), calls=%async_computation.1 | async-start | bytes 425984 | tf_op jit(solution)/shard_map/all_to_all | solution.py:304
  47.5 17.4 %collective-permute-start = (bf16[8,384]{1,0:T(8,128)(2,1)S(1)}, bf16[8,384]{1,0:T(8,128)(2,1)S(1)}, u32[]{:S(2)}, u32[]{:S(2)}) collective-permute-start(bf16[8,384]{1,0:T(8,128)(2,1)S(1)} %slice.6), channel_id=1, source_target_pairs={{0,8},{8,16},{16,24},{24,32},{32,40},{40,48},{48,56},{56,64},{64,7... | collective-permute-start | bytes 18440 | tf_op jit(solution)/shard_map/ppermute | solution.py:310
  64.8 19.3 %copy-start.7 = (bf16[8,384]{1,0:T(8,128)(2,1)}, bf16[8,384]{1,0:T(8,128)(2,1)S(1)}, u32[]{:S(2)}) copy-start(bf16[8,384]{1,0:T(8,128)(2,1)S(1)} %collective-permute-done.before) | copy-start | bytes 18436
  81.6 0.7 copy-start.2
  112.2 37.4 %all-to-all-start.4 = ((f32[8,4,384]{2,1,0:T(4,128)}), f32[8,4,384]{2,1,0:T(4,128)S(1)}, u32[]{:S(2)}, u32[]{:S(2)}) async-start(f32[8,4,384]{2,1,0:T(4,128)} %broadcast_in_dim.2), calls=%async_computation.4 | async-start | bytes 98304 | tf_op jit(solution)/shard_map/all_to_all | solution.py:304
  116.9 7.6 %collective-permute-start.1 = (bf16[8,384]{1,0:T(8,128)(2,1)S(1)}, bf16[8,384]{1,0:T(8,128)(2,1)S(1)}, u32[]{:S(2)}, u32[]{:S(2)}) collective-permute-start(bf16[8,384]{1,0:T(8,128)(2,1)S(1)} %slice.7), channel_id=1, source_target_pairs={{8,0},{16,8},{24,16},{32,24},{40,32},{48,40},{56,48},{64,56},{72,6... | collective-permute-start | bytes 18440 | tf_op jit(solution)/shard_map/ppermute | solution.py:310
  124.5 0.6 copy-start.8
  126.8 3.3 %collective-permute-start.2 = (bf16[4,16,384]{2,1,0:T(8,128)(2,1)}, bf16[4,16,384]{2,1,0:T(8,128)(2,1)S(1)}, u32[]{:S(2)}, u32[]{:S(2)}) collective-permute-start(bf16[4,16,384]{2,1,0:T(8,128)(2,1)} %get-tuple-element.46), channel_id=1, source_target_pairs={{0,1},{1,0},{2,3},{3,2},{4,5},{5,4},{6,7},{7,6},{8,9},{9,8},{10,11... | collective-permute-start | bytes 147464 | tf_op jit(solution)/shard_map/ppermute | solution.py:346
  130.1 0.6 copy-start.3
  132.2 10.4 %collective-permute-start.3 = (bf16[2,16,384]{2,1,0:T(8,128)(2,1)}, bf16[2,16,384]{2,1,0:T(8,128)(2,1)S(1)}, u32[]{:S(2)}, u32[]{:S(2)}) collective-permute-start(bf16[2,16,384]{2,1,0:T(8,128)(2,1)} %get-tuple-element.47), channel_id=1, source_target_pairs={{0,2},{1,3},{2,0},{3,1},{4,6},{5,7},{6,4},{7,5},{8,10},{9,11},{10,... | collective-permute-start | bytes 73736 | tf_op jit(solution)/shard_map/ppermute | solution.py:349
  135.6 7.4 %collective-permute-start.4 = (bf16[2,16,384]{2,1,0:T(8,128)(2,1)}, bf16[2,16,384]{2,1,0:T(8,128)(2,1)S(1)}, u32[]{:S(2)}, u32[]{:S(2)}) collective-permute-start(bf16[2,16,384]{2,1,0:T(8,128)(2,1)} %get-tuple-element.48), channel_id=1, source_target_pairs={{0,4},{1,5},{2,6},{3,7},{4,0},{5,1},{6,2},{7,3},{8,12},{9,13},{10,... | collective-permute-start | bytes 73736 | tf_op jit(solution)/shard_map/ppermute | solution.py:349
  140.3 7.1 %collective-permute-start.5 = (bf16[2,16,384]{2,1,0:T(8,128)(2,1)}, bf16[2,16,384]{2,1,0:T(8,128)(2,1)S(1)}, u32[]{:S(2)}, u32[]{:S(2)}) collective-permute-start(bf16[2,16,384]{2,1,0:T(8,128)(2,1)} %get-tuple-element.49), channel_id=1, source_target_pairs={{0,6},{1,7},{2,4},{3,5},{4,2},{5,3},{6,0},{7,1},{8,14},{9,15},{10,... | collective-permute-start | bytes 73736 | tf_op jit(solution)/shard_map/ppermute | solution.py:349
  142.7 4.7 %copy-start.4 = (bf16[2,16,384]{2,1,0:T(8,128)(2,1)}, bf16[2,16,384]{2,1,0:T(8,128)(2,1)S(1)}, u32[]{:S(2)}) copy-start(bf16[2,16,384]{2,1,0:T(8,128)(2,1)S(1)} %collective-permute-done.3.refs_0_) | copy-start | bytes 73732
  143.0 4.4 %copy-start.5 = (bf16[2,16,384]{2,1,0:T(8,128)(2,1)}, bf16[2,16,384]{2,1,0:T(8,128)(2,1)S(1)}, u32[]{:S(2)}) copy-start(bf16[2,16,384]{2,1,0:T(8,128)(2,1)S(1)} %collective-permute-done.4.refs_1_) | copy-start | bytes 73732
  147.4 0.6 copy-start.6

commit v5 on v4

--- a/solution.py
+++ b/solution.py
@@ -196,14 +196,16 @@
     return grad_q.astype(BF16), grad_k, jnp.concatenate(grad_v, axis=0), gate, tail, states[2]
 
 
-def final_of(end, values, key_rows, tail, grad_k, grad_v, gate, last):
+def value_of(end, key_rows, tail, grad_v):
+    return (grad_v + dot_left(key_rows.astype(F32) * tail, end)).astype(BF16)
+
+
+def keys_of(end, values, key_rows, tail, grad_k, gate, last):
     added = tail * dot(values, end, 1, 1)
-    k = key_rows.astype(F32)
-    grad_value = grad_v + dot_left(k * tail, end)
     upper = ordered(LEN, lambda r, c: r <= c).astype(F32).astype(BF16)
     own = dot_right(jnp.ones((8, WIDTH), BF16), end.astype(F32) * last, 1, 1)[:1]
-    gate = gate - dot_right(upper, k * added) + own
-    return (grad_k + added).astype(BF16), grad_value.astype(BF16), gate.astype(BF16)
+    gate = gate - dot_right(upper, key_rows.astype(F32) * added) + own
+    return (grad_k + added).astype(BF16), gate.astype(BF16)
 
 
 def push_kernel(queries, log_gates, grad_output, out):
@@ -233,25 +235,31 @@
         last[h] = results[5]
 
 
-def final_kernel(
-    ends, values, key_rows, tail, grad_k, grad_v, gate, last, inputs, before, out_k, out_gate, out_v, taps, padded
-):
+def end_of(every, h):
+    return every[:, 8 * h : 8 * h + 8].reshape(LEN, WIDTH).astype(BF16)
+
+
+def value_kernel(ends, key_rows, tail, grad_v, inputs, before, out_v, taps, padded):
     padded[:8] = before[...].astype(F32)
     padded[8:] = inputs[...].astype(F32)
     every = ends[...].astype(F32)
     for h in range(HEADS):
         at = slice(h * WIDTH, (h + 1) * WIDTH)
-        end = every[:, 8 * h : 8 * h + 8].reshape(LEN, WIDTH).astype(BF16)
-        grad_key, grad_value, grad_gate = final_of(
-            end, values[:, at], key_rows[:, at], tail[:, at], grad_k[:, at], grad_v[:, at], gate[:, at], last[h]
-        )
-        out_k[:, at] = grad_key
+        grad_value = value_of(end_of(every, h), key_rows[:, at], tail[:, at], grad_v[:, at])
         out_v[:, at] = grad_value
-        out_gate[:, at] = grad_gate
         rounded = grad_value.astype(F32)
         for tap in range(TAPS):
             term = jnp.sum(padded[8 - tap : 8 - tap + LEN, at] * rounded, axis=0, keepdims=True)
             taps[:, tap : tap + 1, at] = jnp.broadcast_to(term[None], (NEAR, 1, WIDTH))
+
+
+def keys_kernel(ends, values, key_rows, tail, grad_k, gate, last, out_k, out_gate):
+    every = ends[...].astype(F32)
+    for h in range(HEADS):
+        at = slice(h * WIDTH, (h + 1) * WIDTH)
+        out_k[:, at], out_gate[:, at] = keys_of(
+            end_of(every, h), values[:, at], key_rows[:, at], tail[:, at], grad_k[:, at], gate[:, at], last[h]
+        )
 
 
 def conv_kernel_body(place, grad_v, after, weights, mine, other, padded, rows):
@@ -327,12 +335,13 @@
     (sent,) = call(ends_kernel, [((NEAR, OWN, WIDTH), BF16)], 1)(place, near, far)
     ends = exchange(sent, GROUP)
     weights = lax.dynamic_slice_in_dim(conv_kernel, lax.axis_index(HEAD) * columns, columns, 1)
-    grad_keys, grad_gates, grad_rows, taps = call(
-        final_kernel,
-        [(wide, BF16), (wide, BF16), (wide, BF16), ((NEAR, TAPS, columns), F32)],
-        scratch=[pltpu.VMEM((LEN + 8, columns), F32)],
-    )(ends, values, key_rows, tail, grad_k, grad_v, gate, last, conv_input, before)
-    taps = jnp.sum(exchange(taps, GROUP), axis=0)
+    grad_rows, taps = call(
+        value_kernel, [(wide, BF16), ((NEAR, TAPS, columns), F32)], scratch=[pltpu.VMEM((LEN + 8, columns), F32)]
+    )(ends, key_rows, tail, grad_v, conv_input, before)
+    grad_keys, grad_gates = call(keys_kernel, [(wide, BF16), (wide, BF16)])(
+        ends, values, key_rows, tail, grad_k, gate, last
+    )
+    taps = jnp.sum(exchange(taps, GROUP), axis=0).astype(BF16)
     summed = exchange(jnp.broadcast_to(taps[None], (FAR, TAPS, columns)), "zh")
     after = passed_along(grad_rows[:8], -1)
     piece = (LEN // PEERS, columns)
@@ -349,7 +358,7 @@
         lax.ppermute(sent[r - 1], HEAD, [(i, i ^ (2 * r)) for i in range(PEERS)]) for r in range(1, half)
     ]
     (grad_input,) = call(join_kernel, [((LEN // PEERS, PEERS * columns), BF16)], 1)(place, mine, other, *pieces)
-    grad_kernel = jnp.sum(summed, axis=0)
+    grad_kernel = jnp.sum(summed.astype(F32), axis=0)
     return (grad_queries, grad_keys, grad_gates, grad_input, grad_kernel)
 
 

time: 151 us -> 144 us (0.954)
  blocking collectives: 24.6 us -> 12.9 us
  starting transfers between devices: 59.2 us -> 61.7 us
  Pallas kernels: 20.1 us -> 22.1 us
    all_to_all x2 -> x1, blocking collectives: 24.6 us -> 12.9 us  [exchange(): return lax.all_to_all(x, axis, 0, 0, tiled=True)]
    all_to_all x3 -> x4, starting transfers between devices: 38.6 us -> 44.4 us  [exchange(): return lax.all_to_all(x, axis, 0, 0, tiled=True)]
    all_to_all x3 -> x4, waiting for transfers between devices: 23.2 us -> 26.6 us  [exchange(): return lax.all_to_all(x, axis, 0, 0, tiled=True)]
    ppermute x2, starting transfers between devices: 8.29 us -> 4.98 us  [passed_along(): return lax.ppermute(x, SEQ, pairs)]
    ppermute x3, waiting for transfers between devices: 4.73 us -> 2.06 us  [per_device(): lax.ppermute(sent[r - 1], HEAD, [(i, i ^ 2 * r) for i in range(PEERS)])]
    pallas_call x8 -> x9, Pallas kernels: 20.1 us -> 22.1 us  [run(): pl.pallas_call(kernel, out_shape=shapes, in_specs=[pl.BlockSpec(memory_sp...]
  transfers between devices with their start and end apart: 9 -> 10, of which waited for: 7 -> 6; matrix products, arithmetic and copies ran while one was open for 2% -> 2% of each run, Pallas kernels for 8% -> 10%
where the time goes in v5:
time: 144 us; the launch traced here: 143 us
  starting transfers between devices  61.7 us (43%)
  waiting for transfers between devices  38.4 us (27%)
  Pallas kernels  22.1 us (15%)
  blocking collectives  12.9 us (9%)
  local copies, waits for them, and re-layouts  5.76 us (4%)
    all_to_all x4, starting transfers between devices, exchange(): return lax.all_to_all(x, axis, 0, 0, tiled=True)  44.4 us
    all_to_all x4, waiting for transfers between devices, exchange(): return lax.all_to_all(x, axis, 0, 0, tiled=True)  26.6 us
    pallas_call x9, Pallas kernels, run(): pl.pallas_call(kernel, out_shape=shapes, in_specs=[pl.BlockSpec(memory_sp...  22.1 us
    all_to_all x1, blocking collectives, exchange(): return lax.all_to_all(x, axis, 0, 0, tiled=True)  12.9 us
    ppermute x3, starting transfers between devices, per_device(): lax.ppermute(sent[r - 1], HEAD, [(i, i ^ 2 * r) for i in range(PEERS)])  10.4 us
    ppermute x2, waiting for transfers between devices, passed_along(): return lax.ppermute(x, SEQ, pairs)  8.39 us
    ppermute x2, starting transfers between devices, passed_along(): return lax.ppermute(x, SEQ, pairs)  4.98 us
    unnamed x18, local copies, waits for them, and re-layouts  3.16 us
  transfers between devices with their start and end apart: 10, of which 6 were waited for; matrix products, arithmetic and copies ran while one was open for 2% of the time, Pallas kernels for 10%

profile of v5, /device:TPU:8, one launch (start us, length us, event | category | flops | bytes accessed | tf_op | source)
XLA Modules:
  0.0 142.8 jit_solution(16806219849539863451)
XLA Ops:
  0.6 2.1 %shard_map.119 = bf16[16,32,128]{2,1,0:T(8,128)(2,1)} custom-call(bf16[128,384]{1,0:T(8,128)(2,1)} %queries.3, bf16[128,384]{1,0:T(8,128)(2,1)} %log_gates.3, bf16[128,384]{1,0:T(8,128)(2,1)} %grad_output.3), custom_call_target="tpu_custom_call" | custom-call | tf_op jit(solution)/shard_map/pallas_call | solution.py:300
  2.7 16.4 %all-to-all-start = ((bf16[16,32,128]{2,1,0:T(8,128)(2,1)}), bf16[16,32,128]{2,1,0:T(8,128)(2,1)S(1)}, u32[]{:S(2)}, u32[]{:S(2)}) async-start(bf16[16,32,128]{2,1,0:T(8,128)(2,1)} %shard_map.119), calls=%async_computation | async-start | bytes 262144 | tf_op jit(solution)/shard_map/all_to_all | solution.py:312
  19.1 0.6 pad_add_fusion.place
  19.7 6.5 %all-to-all-done.got.near = bf16[16,32,128]{2,1,0:T(8,128)(2,1)S(1)} async-done(((bf16[16,32,128]{2,1,0:T(8,128)(2,1)}), bf16[16,32,128]{2,1,0:T(8,128)(2,1)S(1)}, u32[]{:S(2)}, u32[]{:S(2)}) %all-to-all-start) | async-done | bytes 131104 | tf_op jit(solution)/shard_map/all_to_all | solution.py:312
  26.2 0.6 copy-done.1
  26.9 1.7 %shard_map.121 = bf16[8,104,128]{2,1,0:T(8,128)(2,1)} custom-call(s32[3]{0:T(128)} %pad_add_fusion.place, bf16[16,32,128]{2,1,0:T(8,128)(2,1)} %copy-done.1), custom_call_target="tpu_custom_call" | custom-call | tf_op jit(solution)/shard_map/pallas_call | solution.py:300
  28.6 18.2 %all-to-all-start.1 = ((bf16[8,104,128]{2,1,0:T(8,128)(2,1)}), bf16[8,104,128]{2,1,0:T(8,128)(2,1)S(1)}, u32[]{:S(2)}, u32[]{:S(2)}) async-start(bf16[8,104,128]{2,1,0:T(8,128)(2,1)} %shard_map.121), calls=%async_computation.1 | async-start | bytes 425984 | tf_op jit(solution)/shard_map/all_to_all | solution.py:312
  46.8 0.7 slice.6
  47.5 2.0 %collective-permute-start = (bf16[8,384]{1,0:T(8,128)(2,1)S(1)}, bf16[8,384]{1,0:T(8,128)(2,1)S(1)}, u32[]{:S(2)}, u32[]{:S(2)}) collective-permute-start(bf16[8,384]{1,0:T(8,128)(2,1)S(1)} %slice.6), channel_id=1, source_target_pairs={{0,8},{8,16},{16,24},{24,32},{32,40},{40,48},{48,56},{56,64},{64,7... | collective-permute-start | bytes 18440 | tf_op jit(solution)/shard_map/ppermute | solution.py:318
  49.5 6.9 %shard_map.120 = (bf16[128,384]{1,0:T(8,128)(2,1)}, f32[128,384]{1,0:T(8,128)}, f32[128,384]{1,0:T(8,128)}, f32[128,384]{1,0:T(8,128)}, f32[128,384]{1,0:T(8,128)}, /*index=5*/f32[3,128,128]{2,1,0:T(8,128)}) custom-call(bf16[128,384]{1,0:T(8,128)(2,1)} %queries.3, bf16[128,384]{1,0:T(8,128)(2,1)} %key_rows.5, bf16[128,384]{1,0:T(8,128)(2,1)} %values.3, ...), custom_call_target="tpu_custom_call" | custom-call | tf_op jit(solution)/shard_map/pallas_call | solution.py:300
  56.4 8.4 %collective-permute-done.before = bf16[8,384]{1,0:T(8,128)(2,1)S(1)} collective-permute-done((bf16[8,384]{1,0:T(8,128)(2,1)S(1)}, bf16[8,384]{1,0:T(8,128)(2,1)S(1)}, u32[]{:S(2)}, u32[]{:S(2)}) %collective-permute-start) | collective-permute-done | bytes 6176 | tf_op jit(solution)/shard_map/ppermute | solution.py:318
  64.8 16.7 %all-to-all-done.1.far = bf16[8,104,128]{2,1,0:T(8,128)(2,1)S(1)} async-done(((bf16[8,104,128]{2,1,0:T(8,128)(2,1)}), bf16[8,104,128]{2,1,0:T(8,128)(2,1)S(1)}, u32[]{:S(2)}, u32[]{:S(2)}) %all-to-all-start.1) | async-done | bytes 213024 | tf_op jit(solution)/shard_map/all_to_all | solution.py:312
  81.6 0.7 copy-done.2
  82.2 1.9 %shard_map.122 = bf16[16,24,128]{2,1,0:T(8,128)(2,1)} custom-call(s32[3]{0:T(128)} %pad_add_fusion.place, bf16[16,32,128]{2,1,0:T(8,128)(2,1)} %copy-done.1, bf16[8,104,128]{2,1,0:T(8,128)(2,1)} %copy-done.2), custom_call_target="tpu_custom_call" | custom-call | tf_op jit(solution)/shard_map/pallas_call | solution.py:300
  84.1 12.9 %all_to_all.25.ends = bf16[16,24,128]{2,1,0:T(8,128)(2,1)} all-to-all(bf16[16,24,128]{2,1,0:T(8,128)(2,1)} %shard_map.122), channel_id=1, replica_groups=mesh['y'=4,'zh'=8,'zl'=4,'x'=4,'core'=2] {'y','zl'}, dimensions={0} | all-to-all | bytes 196608 | tf_op jit(solution)/shard_map/all_to_all | solution.py:312
  97.0 2.2 %shard_map.124 = (bf16[128,384]{1,0:T(8,128)(2,1)}, f32[16,4,384]{2,1,0:T(4,128)}) custom-call(bf16[16,24,128]{2,1,0:T(8,128)(2,1)} %all_to_all.25.ends, bf16[128,384]{1,0:T(8,128)(2,1)} %key_rows.5, f32[128,384]{1,0:T(8,128)} %get-tuple-element.36.tail, f32[128,384]{1,0:T(8,128)} %get-tuple-element.42.grad_v, bf16[128,384]{1,0:T(8,128)(2,1)} %inputs.1, ...), custom_call_target="tpu_custom_call" | custom-call | tf_op jit(solution)/shard_map/pallas_call | solution.py:300
  99.2 4.8 %all-to-all-start.3 = ((f32[16,4,384]{2,1,0:T(4,128)}), f32[16,4,384]{2,1,0:T(4,128)S(1)}, u32[]{:S(2)}, u32[]{:S(2)}) async-start(f32[16,4,384]{2,1,0:T(4,128)} %get-tuple-element.50), calls=%async_computation.3 | async-start | bytes 196608 | tf_op jit(solution)/shard_map/all_to_all | solution.py:312
  103.9 0.7 slice.7
  104.6 3.0 %collective-permute-start.1 = (bf16[8,384]{1,0:T(8,128)(2,1)S(1)}, bf16[8,384]{1,0:T(8,128)(2,1)S(1)}, u32[]{:S(2)}, u32[]{:S(2)}) collective-permute-start(bf16[8,384]{1,0:T(8,128)(2,1)S(1)} %slice.7), channel_id=1, source_target_pairs={{8,0},{16,8},{24,16},{32,24},{40,32},{48,40},{56,48},{64,56},{72,6... | collective-permute-start | bytes 18440 | tf_op jit(solution)/shard_map/ppermute | solution.py:318
  107.6 3.3 %all-to-all-done.3 = f32[16,4,384]{2,1,0:T(4,128)S(1)} async-done(((f32[16,4,384]{2,1,0:T(4,128)}), f32[16,4,384]{2,1,0:T(4,128)S(1)}, u32[]{:S(2)}, u32[]{:S(2)}) %all-to-all-start.3) | async-done | bytes 98336 | tf_op jit(solution)/shard_map/all_to_all | solution.py:312
  111.5 5.1 %all-to-all-start.4 = ((bf16[8,4,384]{2,1,0:T(4,128)(2,1)}), bf16[8,4,384]{2,1,0:T(4,128)(2,1)S(1)}, u32[]{:S(2)}, u32[]{:S(2)}) async-start(bf16[8,4,384]{2,1,0:T(4,128)(2,1)} %broadcast_in_dim.2), calls=%async_computation.4 | async-start | bytes 49152 | tf_op jit(solution)/shard_map/all_to_all | solution.py:312
  117.8 1.7 %shard_map.125 = (bf16[4,16,384]{2,1,0:T(8,128)(2,1)}, bf16[4,16,384]{2,1,0:T(8,128)(2,1)}) custom-call(s32[3]{0:T(128)} %pad_add_fusion.place, bf16[128,384]{1,0:T(8,128)(2,1)} %get-tuple-element.44.grad_v, bf16[8,384]{1,0:T(8,128)(2,1)} %copy-done.8, f32[4,384]{1,0:T(4,128)} %constant_dynamic-slice_fusion.weights), custom_call_target="tpu_custom_call" | custom-call | tf_op jit(solution)/shard_map/pallas_call | solution.py:300
  119.5 1.9 %collective-permute-start.2 = (bf16[4,16,384]{2,1,0:T(8,128)(2,1)}, bf16[4,16,384]{2,1,0:T(8,128)(2,1)S(1)}, u32[]{:S(2)}, u32[]{:S(2)}) collective-permute-start(bf16[4,16,384]{2,1,0:T(8,128)(2,1)} %get-tuple-element.46), channel_id=1, source_target_pairs={{0,1},{1,0},{2,3},{3,2},{4,5},{5,4},{6,7},{7,6},{8,9},{9,8},{10,11... | collective-permute-start | bytes 147464 | tf_op jit(solution)/shard_map/ppermute | solution.py:355
  121.4 1.4 collective-permute-done.2.other
  123.5 1.4 %shard_map.126 = (bf16[2,16,384]{2,1,0:T(8,128)(2,1)}, bf16[2,16,384]{2,1,0:T(8,128)(2,1)}, bf16[2,16,384]{2,1,0:T(8,128)(2,1)}) custom-call(bf16[4,16,384]{2,1,0:T(8,128)(2,1)} %get-tuple-element.45.mine, bf16[4,16,384]{2,1,0:T(8,128)(2,1)} %copy-done.3), custom_call_target="tpu_custom_call" | custom-call | tf_op jit(solution)/shard_map/pallas_call | solution.py:300
  124.9 3.4 %collective-permute-start.3 = (bf16[2,16,384]{2,1,0:T(8,128)(2,1)}, bf16[2,16,384]{2,1,0:T(8,128)(2,1)S(1)}, u32[]{:S(2)}, u32[]{:S(2)}) collective-permute-start(bf16[2,16,384]{2,1,0:T(8,128)(2,1)} %get-tuple-element.47), channel_id=1, source_target_pairs={{0,2},{1,3},{2,0},{3,1},{4,6},{5,7},{6,4},{7,5},{8,10},{9,11},{10,... | collective-permute-start | bytes 73736 | tf_op jit(solution)/shard_map/ppermute | solution.py:358
  128.3 4.6 %collective-permute-start.4 = (bf16[2,16,384]{2,1,0:T(8,128)(2,1)}, bf16[2,16,384]{2,1,0:T(8,128)(2,1)S(1)}, u32[]{:S(2)}, u32[]{:S(2)}) collective-permute-start(bf16[2,16,384]{2,1,0:T(8,128)(2,1)} %get-tuple-element.48), channel_id=1, source_target_pairs={{0,4},{1,5},{2,6},{3,7},{4,0},{5,1},{6,2},{7,3},{8,12},{9,13},{10,... | collective-permute-start | bytes 73736 | tf_op jit(solution)/shard_map/ppermute | solution.py:358
  132.9 2.4 %collective-permute-start.5 = (bf16[2,16,384]{2,1,0:T(8,128)(2,1)}, bf16[2,16,384]{2,1,0:T(8,128)(2,1)S(1)}, u32[]{:S(2)}, u32[]{:S(2)}) collective-permute-start(bf16[2,16,384]{2,1,0:T(8,128)(2,1)} %get-tuple-element.49), channel_id=1, source_target_pairs={{0,6},{1,7},{2,4},{3,5},{4,2},{5,3},{6,0},{7,1},{8,14},{9,15},{10,... | collective-permute-start | bytes 73736 | tf_op jit(solution)/shard_map/ppermute | solution.py:358
  135.3 2.7 %shard_map.123 = (bf16[128,384]{1,0:T(8,128)(2,1)}, bf16[128,384]{1,0:T(8,128)(2,1)}) custom-call(bf16[16,24,128]{2,1,0:T(8,128)(2,1)} %all_to_all.25.ends, bf16[128,384]{1,0:T(8,128)(2,1)} %values.3, bf16[128,384]{1,0:T(8,128)(2,1)} %key_rows.5, f32[128,384]{1,0:T(8,128)} %get-tuple-element.36.tail, f32[128,384]{1,0:T(8,128)} %get-tuple-element.37.grad_k, ...), custom_call_target="tpu_custom_call" | custom-call | tf_op jit(solution)/shard_map/pallas_call | solution.py:300
  138.0 2.1 %collective-permute-done.5.refs_2_ = bf16[2,16,384]{2,1,0:T(8,128)(2,1)S(1)} collective-permute-done((bf16[2,16,384]{2,1,0:T(8,128)(2,1)}, bf16[2,16,384]{2,1,0:T(8,128)(2,1)S(1)}, u32[]{:S(2)}, u32[]{:S(2)}) %collective-permute-start.5) | collective-permute-done | bytes 24608 | tf_op jit(solution)/shard_map/ppermute | solution.py:358
  140.7 1.5 %shard_map.127 = bf16[16,3072]{1,0:T(8,128)(2,1)} custom-call(s32[3]{0:T(128)} %pad_add_fusion.place, bf16[4,16,384]{2,1,0:T(8,128)(2,1)} %get-tuple-element.45.mine, bf16[4,16,384]{2,1,0:T(8,128)(2,1)} %copy-done.3, bf16[2,16,384]{2,1,0:T(8,128)(2,1)} %copy-done.4, bf16[2,16,384]{2,1,0:T(8,128)(2,1)} %copy-done.5, bf16[2,16,384]{2,1,0:T(8,128)(2,1)} %copy-done.6), custom_call_target="tpu_custom_call" | custom-call | tf_op jit(solution)/shard_map/pallas_call | solution.py:300
  142.2 0.6 convert_reduce_fusion
  (23 shorter events, 3.1 us)
Async XLA Ops:
  0.6 116.0 %copy-start = (f32[4,3072]{1,0:T(4,128)S(1)}, f32[4,3072]{1,0:T(4,128)}, u32[]{:S(2)}) copy-start(f32[4,3072]{1,0:T(4,128)} %param.15) | copy-start | bytes 147460
  2.7 23.5 %all-to-all-start = ((bf16[16,32,128]{2,1,0:T(8,128)(2,1)}), bf16[16,32,128]{2,1,0:T(8,128)(2,1)S(1)}, u32[]{:S(2)}, u32[]{:S(2)}) async-start(bf16[16,32,128]{2,1,0:T(8,128)(2,1)} %shard_map.119), calls=%async_computation | async-start | bytes 262144 | tf_op jit(solution)/shard_map/all_to_all | solution.py:312
  26.2 0.6 copy-start.1
  28.6 53.0 %all-to-all-start.1 = ((bf16[8,104,128]{2,1,0:T(8,128)(2,1)}), bf16[8,104,128]{2,1,0:T(8,128)(2,1)S(1)}, u32[]{:S(2)}, u32[]{:S(2)}) async-start(bf16[8,104,128]{2,1,0:T(8,128)(2,1)} %shard_map.121), calls=%async_computation.1 | async-start | bytes 425984 | tf_op jit(solution)/shard_map/all_to_all | solution.py:312
  47.5 17.4 %collective-permute-start = (bf16[8,384]{1,0:T(8,128)(2,1)S(1)}, bf16[8,384]{1,0:T(8,128)(2,1)S(1)}, u32[]{:S(2)}, u32[]{:S(2)}) collective-permute-start(bf16[8,384]{1,0:T(8,128)(2,1)S(1)} %slice.6), channel_id=1, source_target_pairs={{0,8},{8,16},{16,24},{24,32},{32,40},{40,48},{48,56},{56,64},{64,7... | collective-permute-start | bytes 18440 | tf_op jit(solution)/shard_map/ppermute | solution.py:318
  64.8 19.3 %copy-start.7 = (bf16[8,384]{1,0:T(8,128)(2,1)}, bf16[8,384]{1,0:T(8,128)(2,1)S(1)}, u32[]{:S(2)}) copy-start(bf16[8,384]{1,0:T(8,128)(2,1)S(1)} %collective-permute-done.before) | copy-start | bytes 18436
  81.6 0.7 copy-start.2
  99.2 11.7 %all-to-all-start.3 = ((f32[16,4,384]{2,1,0:T(4,128)}), f32[16,4,384]{2,1,0:T(4,128)S(1)}, u32[]{:S(2)}, u32[]{:S(2)}) async-start(f32[16,4,384]{2,1,0:T(4,128)} %get-tuple-element.50), calls=%async_computation.3 | async-start | bytes 196608 | tf_op jit(solution)/shard_map/all_to_all | solution.py:312
  104.6 12.6 %collective-permute-start.1 = (bf16[8,384]{1,0:T(8,128)(2,1)S(1)}, bf16[8,384]{1,0:T(8,128)(2,1)S(1)}, u32[]{:S(2)}, u32[]{:S(2)}) collective-permute-start(bf16[8,384]{1,0:T(8,128)(2,1)S(1)} %slice.7), channel_id=1, source_target_pairs={{8,0},{16,8},{24,16},{32,24},{40,32},{48,40},{56,48},{64,56},{72,6... | collective-permute-start | bytes 18440 | tf_op jit(solution)/shard_map/ppermute | solution.py:318
  111.5 30.7 %all-to-all-start.4 = ((bf16[8,4,384]{2,1,0:T(4,128)(2,1)}), bf16[8,4,384]{2,1,0:T(4,128)(2,1)S(1)}, u32[]{:S(2)}, u32[]{:S(2)}) async-start(bf16[8,4,384]{2,1,0:T(4,128)(2,1)} %broadcast_in_dim.2), calls=%async_computation.4 | async-start | bytes 49152 | tf_op jit(solution)/shard_map/all_to_all | solution.py:312
  117.2 0.6 copy-start.8
  119.5 3.3 %collective-permute-start.2 = (bf16[4,16,384]{2,1,0:T(8,128)(2,1)}, bf16[4,16,384]{2,1,0:T(8,128)(2,1)S(1)}, u32[]{:S(2)}, u32[]{:S(2)}) collective-permute-start(bf16[4,16,384]{2,1,0:T(8,128)(2,1)} %get-tuple-element.46), channel_id=1, source_target_pairs={{0,1},{1,0},{2,3},{3,2},{4,5},{5,4},{6,7},{7,6},{8,9},{9,8},{10,11... | collective-permute-start | bytes 147464 | tf_op jit(solution)/shard_map/ppermute | solution.py:355
  122.8 0.6 copy-start.3
  124.9 13.1 %collective-permute-start.3 = (bf16[2,16,384]{2,1,0:T(8,128)(2,1)}, bf16[2,16,384]{2,1,0:T(8,128)(2,1)S(1)}, u32[]{:S(2)}, u32[]{:S(2)}) collective-permute-start(bf16[2,16,384]{2,1,0:T(8,128)(2,1)} %get-tuple-element.47), channel_id=1, source_target_pairs={{0,2},{1,3},{2,0},{3,1},{4,6},{5,7},{6,4},{7,5},{8,10},{9,11},{10,... | collective-permute-start | bytes 73736 | tf_op jit(solution)/shard_map/ppermute | solution.py:358
  128.3 9.7 %collective-permute-start.4 = (bf16[2,16,384]{2,1,0:T(8,128)(2,1)}, bf16[2,16,384]{2,1,0:T(8,128)(2,1)S(1)}, u32[]{:S(2)}, u32[]{:S(2)}) collective-permute-start(bf16[2,16,384]{2,1,0:T(8,128)(2,1)} %get-tuple-element.48), channel_id=1, source_target_pairs={{0,4},{1,5},{2,6},{3,7},{4,0},{5,1},{6,2},{7,3},{8,12},{9,13},{10,... | collective-permute-start | bytes 73736 | tf_op jit(solution)/shard_map/ppermute | solution.py:358
  132.9 7.1 %collective-permute-start.5 = (bf16[2,16,384]{2,1,0:T(8,128)(2,1)}, bf16[2,16,384]{2,1,0:T(8,128)(2,1)S(1)}, u32[]{:S(2)}, u32[]{:S(2)}) collective-permute-start(bf16[2,16,384]{2,1,0:T(8,128)(2,1)} %get-tuple-element.49), channel_id=1, source_target_pairs={{0,6},{1,7},{2,4},{3,5},{4,2},{5,3},{6,0},{7,1},{8,14},{9,15},{10,... | collective-permute-start | bytes 73736 | tf_op jit(solution)/shard_map/ppermute | solution.py:358
  138.0 2.1 %copy-start.4 = (bf16[2,16,384]{2,1,0:T(8,128)(2,1)}, bf16[2,16,384]{2,1,0:T(8,128)(2,1)S(1)}, u32[]{:S(2)}) copy-start(bf16[2,16,384]{2,1,0:T(8,128)(2,1)S(1)} %collective-permute-done.3.refs_0_) | copy-start | bytes 73732
  138.0 2.1 %copy-start.5 = (bf16[2,16,384]{2,1,0:T(8,128)(2,1)}, bf16[2,16,384]{2,1,0:T(8,128)(2,1)S(1)}, u32[]{:S(2)}) copy-start(bf16[2,16,384]{2,1,0:T(8,128)(2,1)S(1)} %collective-permute-done.4.refs_1_) | copy-start | bytes 73732
  140.1 0.6 copy-start.6
